TPU v7x, 256 devices: a whole 4x4x8 slice. The times are simulated.
256 devices in a mesh: row: 64 (over y, z, core), col: 4 (over x).
Axes of the slice: x: 4, y: 4, z: 8, core: 2. Of those that a mesh axis runs over, the one named last changes fastest.
Arguments:
- factor: float32 [8192, 8192], P('row', 'col'), may hold values from -0.125 to 0.125
- rhs: float32 [8192, 512], P('row', 'col'), may hold values from -6 to 6
- parent: int32 [7], replicated, may hold values from 4 to 6, as said below
- bounds: int32 [8], replicated, may hold values from 0 to 64, as said below
- slot: int32 [64], replicated, may hold values from 0 to 63, each once
- structure: int32 [7, 64], replicated, may hold values 0 or 1
Outputs:
- solution: float32 [8192, 512], P('row', 'col')
Inputs may be any that keep to these rules, and one draw needn't show every extreme that they name: parent[s] is 4 or 5 for s = 0 to 3, and 6 for s = 4, 5, 6 (the root is its own entry). bounds[0] = 0, bounds[7] = 64, strictly increasing; supernode s holds logical blocks bounds[s] to bounds[s+1] - 1. `slot`: a permutation.
All inputs are finite; a program needn't handle non-finite values.
Results may differ from a plain program's by a relative error of at most 0.0001.
Values sent between devices are 32-bit elements; how exact they have to be, the bound alone decides.
A program may use at most 64 MiB of HBM per device.

v0:
```python
import functools

import jax
import jax.numpy as jnp
from jax import lax
from jax.experimental import pallas as pl
from jax.experimental.pallas import tpu as pltpu
from jax.sharding import PartitionSpec as P

B = 128
RB = 1
MESH = pl.DeviceIdType.MESH
NY, NZ, NC = 4, 8, 2


def block_masks(parent, bounds, slot, structure):
    count = slot.shape[0]
    ar = jnp.arange(count, dtype=jnp.int32)
    logical = jnp.sum(jnp.where(slot[:, None] == ar[None, :], ar[:, None], 0), axis=0)
    node = jnp.sum((logical[:, None] >= bounds[None, 1:7]).astype(jnp.int32), axis=1)
    level = (node >= 4).astype(jnp.int32) + (node >= 6).astype(jnp.int32)
    nodes = jnp.arange(7, dtype=jnp.int32)
    grand = parent[parent]
    ancestor = ((nodes[None, :] == parent[:, None]) | (nodes[None, :] == grand[:, None])) & (
        nodes[None, :] != nodes[:, None]
    )
    node_hot = (node[:, None] == nodes[None, :]).astype(jnp.float32)
    perm_hot = (logical[:, None] == ar[None, :]).astype(jnp.float32)
    listed_store = jnp.dot(
        structure.astype(jnp.float32), perm_hot.T, precision=lax.Precision.HIGHEST
    )
    anc_pairs = jnp.dot(
        node_hot,
        jnp.dot(ancestor.astype(jnp.float32), node_hot.T, precision=lax.Precision.HIGHEST),
        precision=lax.Precision.HIGHEST,
    )
    list_pairs = jnp.dot(node_hot, listed_store, precision=lax.Precision.HIGHEST)
    link = (anc_pairs * list_pairs).T > 0.5
    same = node[:, None] == node[None, :]
    return (level, same, link)


def masked(block_rows, mask):
    rblocks, width = mask.shape
    bsz = block_rows.shape[0] // rblocks
    shaped = block_rows.reshape(rblocks, bsz, width, bsz) * mask[:, None, :, None].astype(
        jnp.float32
    )
    return shaped.reshape(block_rows.shape)


def gather_kernel(*refs, fused):
    if fused:
        x_ref, f_ref, out_ref, G, acc, local_sem, send_sem, recv_z, recv_y, recv_c = refs
    else:
        x_ref, out_ref, G, local_sem, send_sem, recv_z, recv_y, recv_c = refs
    nb = x_ref.shape[0]
    r = lax.axis_index("row")
    c = lax.axis_index("col")
    y = r // (NZ * NC)
    z = (r // NC) % NZ
    k = r % NC

    def dev(yy, zz, kk):
        return (((yy + NY) % NY) * NZ + (zz + NZ) % NZ) * NC + kk

    def slot(yy, zz, kk):
        return kk * (NY * NZ) + ((yy + NY) % NY) * NZ + (zz + NZ) % NZ

    def rows(first, n=1):
        return G.at[pl.ds(pl.multiple_of(first * nb, nb), n * nb)]

    zr, zl = dev(y, z + 1, k), dev(y, z - 1, k)
    yr, yl = dev(y + 1, z, k), dev(y - 1, z, k)
    partner = dev(y, z, 1 - k)

    barrier = pltpu.get_barrier_semaphore()
    for d in (zr, zl, yr, yl, partner):
        pl.semaphore_signal(barrier, inc=1, device_id=(d, c), device_id_type=MESH)
    pl.semaphore_wait(barrier, 5)

    own = slot(y, z, k)
    local = pltpu.make_async_copy(x_ref, rows(own), local_sem.at[0])
    local.start()
    if fused:
        acc[...] = jnp.zeros_like(acc)

    sends = []

    def remote(src, dst, si, rsem, d):
        return pltpu.make_async_remote_copy(
            src_ref=src, dst_ref=dst, send_sem=send_sem.at[si], recv_sem=rsem,
            device_id=(d, c), device_id_type=MESH,
        )

    def send(src, dst, rsem, d):
        cp = remote(src, dst, len(sends), rsem, d)
        cp.start()
        sends.append(cp)

    def wait_z(zsrc):
        remote(x_ref, rows(slot(y, zsrc, k)), 0, recv_z.at[(zsrc + NZ) % NZ], zr).wait_recv()

    def chunk_start(kk, yy):
        return kk * (NY * NZ) + ((yy + NY) % NY) * NZ

    def chunk(kk, yy, lo=0, n=NZ):
        return rows(chunk_start(kk, yy) + lo, n)

    def multiply(kk, yy):
        if fused:
            s0 = chunk_start(kk, yy)
            cols = pl.ds(pl.multiple_of(s0 * nb, nb), NZ * nb)
            acc[...] += jnp.dot(
                f_ref[:, cols], G[cols, :],
                precision=lax.Precision.HIGHEST, preferred_element_type=jnp.float32,
            )

    for s in range(4):
        if s >= 1:
            wait_z(z - s)
        src = x_ref if s == 0 else rows(slot(y, z - s, k))
        send(src, rows(slot(y, z - s, k)), recv_z.at[(z - s + NZ) % NZ], zr)
        if s < 3:
            if s >= 1:
                wait_z(z + s)
            src = x_ref if s == 0 else rows(slot(y, z + s, k))
            send(src, rows(slot(y, z + s, k)), recv_z.at[(z + s) % NZ], zl)
    wait_z(z - 4)
    wait_z(z + 3)
    local.wait()

    half = NZ // 2
    send(chunk(k, y), chunk(k, y), recv_y.at[0], yr)
    send(chunk(k, y), chunk(k, y), recv_y.at[1], yl)
    send(chunk(k, y), chunk(k, y), recv_c.at[0], partner)
    multiply(k, y)
    remote(chunk(k, y - 1), chunk(k, y - 1), 0, recv_y.at[0], yr).wait_recv()
    send(chunk(k, y - 1, 0, half), chunk(k, y - 1, 0, half), recv_y.at[2], yr)
    send(chunk(k, y - 1), chunk(k, y - 1), recv_c.at[3], partner)
    remote(chunk(k, y + 1), chunk(k, y + 1), 0, recv_y.at[1], yl).wait_recv()
    send(chunk(k, y + 1, half, half), chunk(k, y + 1, half, half), recv_y.at[3], yl)
    send(chunk(k, y + 1), chunk(k, y + 1), recv_c.at[1], partner)
    multiply(k, y - 1)
    multiply(k, y + 1)
    remote(chunk(k, y + 2, 0, half), chunk(k, y + 2, 0, half), 0, recv_y.at[2], yr).wait_recv()
    remote(chunk(k, y + 2, half, half), chunk(k, y + 2, half, half), 0, recv_y.at[3], yl).wait_recv()
    send(chunk(k, y + 2), chunk(k, y + 2), recv_c.at[2], partner)
    multiply(k, y + 2)

    for d in (0, 3, 1, 2):
        remote(chunk(1 - k, y + d), chunk(1 - k, y + d), 0, recv_c.at[d], partner).wait_recv()
        multiply(1 - k, y + d)

    for cp in sends:
        cp.wait_send()
    if fused:
        out_ref[...] = acc[...]
    else:
        out_ref[...] = G[...]


def _sems():
    return [
        pltpu.SemaphoreType.DMA((1,)),
        pltpu.SemaphoreType.DMA((16,)),
        pltpu.SemaphoreType.DMA((NZ,)),
        pltpu.SemaphoreType.DMA((4,)),
        pltpu.SemaphoreType.DMA((4,)),
    ]


def gather_rows(x, cid):
    nb, w = x.shape
    n = NY * NZ * NC
    return pl.pallas_call(
        functools.partial(gather_kernel, fused=False),
        out_shape=jax.ShapeDtypeStruct((n * nb, w), x.dtype),
        in_specs=[pl.BlockSpec(memory_space=pltpu.VMEM)],
        out_specs=pl.BlockSpec(memory_space=pltpu.VMEM),
        scratch_shapes=[pltpu.VMEM((n * nb, w), x.dtype)] + _sems(),
        compiler_params=pltpu.CompilerParams(collective_id=cid, has_side_effects=True),
        cost_estimate=pl.CostEstimate(flops=0, transcendentals=0, bytes_accessed=2 * n * nb * w * 4),
    )(x)


def gather_product(matrix, x, cid):
    nb, w = x.shape
    n = NY * NZ * NC
    return pl.pallas_call(
        functools.partial(gather_kernel, fused=True),
        out_shape=jax.ShapeDtypeStruct((matrix.shape[0], w), jnp.float32),
        in_specs=[pl.BlockSpec(memory_space=pltpu.VMEM)] * 2,
        out_specs=pl.BlockSpec(memory_space=pltpu.VMEM),
        scratch_shapes=[pltpu.VMEM((n * nb, w), x.dtype), pltpu.VMEM((matrix.shape[0], w), jnp.float32)]
        + _sems(),
        compiler_params=pltpu.CompilerParams(collective_id=cid, has_side_effects=True),
        cost_estimate=pl.CostEstimate(
            flops=2 * matrix.shape[0] * matrix.shape[1] * w, transcendentals=0,
            bytes_accessed=(matrix.size + 2 * n * nb * w) * 4,
        ),
    )(x, matrix)


def to_slot_order(cols):
    rows = cols.shape[0]
    return cols.reshape(rows, NY * NZ, NC, B).transpose(0, 2, 1, 3).reshape(rows, -1)


def body(factor, rhs, parent, bounds, slot, structure):
    level, same, link = block_masks(parent, bounds, slot, structure)
    first = lax.axis_index("row") * RB
    level_mine = lax.dynamic_slice_in_dim(level, first, RB, 0)
    same_mine = lax.dynamic_slice_in_dim(same, first, RB, 0)
    link_mine = lax.dynamic_slice_in_dim(link, first, RB, 0)
    full_rows = lax.all_gather(factor, "col", axis=1, tiled=True)
    diag_part = to_slot_order(masked(full_rows, same_mine))
    link_part = to_slot_order(masked(full_rows, link_mine))

    calls = [0]

    def product(matrix, vector):
        cid = calls[0]
        calls[0] += 1
        if cid == 0:
            return jnp.dot(
                matrix,
                gather_rows(vector, cid),
                precision=lax.Precision.HIGHEST,
                preferred_element_type=jnp.float32,
            )
        return gather_product(matrix, vector, cid)

    pieces = [rhs]
    accums = [jnp.zeros(p.shape, jnp.float32) for p in pieces]
    results = [jnp.zeros(p.shape, jnp.float32) for p in pieces]
    for section in range(3):
        rows = jnp.repeat(level_mine == section, B)[:, None]
        solved = jnp.where(rows, product(diag_part, pieces[0] - accums[0]), 0.0)
        results[0] = results[0] + solved
        if section < 2:
            accums[0] = accums[0] + product(link_part, solved)
    return results[0]


def solution(mesh):
    in_specs = (P("row", "col"), P("row", "col"), P(), P(), P(), P())
    out_specs = P("row", "col")
    return jax.shard_map(body, mesh=mesh, in_specs=in_specs, out_specs=out_specs, check_vma=False)
```

profile of v0, /device:TPU:1, one launch (start us, length us, event | category | flops | bytes accessed | tf_op | source)
XLA Modules:
  0.0 269.0 jit_solution(14256949511405357375)
XLA Ops:
  6.5 0.0 all-gather.2.cloned.1.call-start
  6.5 0.7 all-gather.2.cloned.1.call-update
  7.3 0.7 slice.3
  8.0 0.7 compare_select_fusion
  8.7 1.3 gather_fusion
  9.9 0.8 select_reduce_fusion
  10.7 0.1 convert_reduce_fusion
  10.8 0.6 dynamic-slice
  11.4 0.8 fusion.2
  12.2 0.9 fusion.3
  13.1 0.3 fusion.1
  13.4 0.2 fusion
  13.6 0.7 fusion.15
  14.3 0.1 reshape.57
  14.4 0.1 copy.15
  14.5 0.1 reshape.58
  14.6 0.1 copy.17
  14.7 0.6 dynamic_slice.9
  15.3 45.1 %shard_map.64 = f32[8192,128]{1,0:T(8,128)} custom-call(f32[128,128]{1,0:T(8,128)} %refs_0_.1), custom_call_target="tpu_custom_call" | custom-call | bytes 8388608 | tf_op jit(solution)/shard_map/pallas_call | solution.py:176
  62.3 1.5 all-gather.2.cloned.1.call-done
  63.8 6.8 %reshape.54 = f32[128,32,2,128]{3,2,1,0:T(2,128)} reshape(f32[128,8192]{1,0:T(8,128)} %all-gather.2.cloned.1.call-done) | data formatting | bytes 8388608 | tf_op jit(solution)/shard_map/reshape | solution.py:46
  70.7 3.4 %copy_multiply_fusion = (f32[128,32,2,128]{3,1,2,0:T(8,128)S(1)}, f32[128,32,2,128]{3,1,2,0:T(8,128)S(1)}) fusion(f32[128,32,2,128]{3,2,1,0:T(2,128)} %reshape.54, f32[32,2]{0,1:T(2,128)S(1)} %copy.17, f32[32,2]{0,1:T(2,128)S(1)} %copy.15), kind=kLoop, calls=%fused_computation.3 | loop fusion | flops 2097152 | bytes 12583424 | tf_op jit(solution)/shard_map/mul | solution.py:46
  74.1 5.3 %copy.26 = f32[16,8,64,128]{3,1,2,0:T(8,128)} copy(f32[16,8,64,128]{3,2,1,0:T(8,128)S(1)} %bitcast.25) | data formatting | bytes 8388608
  79.3 0.0 copy-start
  79.3 5.2 %copy.27 = f32[16,8,64,128]{3,1,2,0:T(8,128)} copy(f32[16,8,64,128]{3,2,1,0:T(8,128)S(1)} %bitcast.23) | data formatting | bytes 8388608
  84.6 0.0 copy-done
  84.6 7.6 %convolution_select_fusion.refs_0_ = f32[128,128]{1,0:T(8,128)} fusion(f32[8192,128]{1,0:T(8,128)S(1)} %copy-done, pred[]{:T(512)} %bitcast, f32[16,8,64,128]{3,2,1,0:T(8,128)S(1)} %bitcast.24), kind=kOutput, calls=%fused_computation.5 | convolution fusion | flops 1610629120 | bytes 8454145 | tf_op jit(solution)/shard_map/dot_general | solution.py:226
  92.2 0.0 copy-start.2
  92.2 43.3 %shard_map.65 = f32[128,128]{1,0:T(8,128)} custom-call(f32[128,128]{1,0:T(8,128)} %convolution_select_fusion.refs_0_, f32[128,8192]{1,0:T(8,128)} %bitcast.21), custom_call_target="tpu_custom_call" | custom-call | flops 268435456 | bytes 12582912 | tf_op jit(solution)/shard_map/pallas_call | solution.py:190
  135.5 0.0 copy-done.2
  135.5 1.5 sub.6.refs_0_
  137.0 0.0 copy-start.3
  137.0 37.4 %shard_map.66 = f32[128,128]{1,0:T(8,128)} custom-call(f32[128,128]{1,0:T(8,128)} %sub.6.refs_0_, f32[128,8192]{1,0:T(8,128)} %bitcast.19), custom_call_target="tpu_custom_call" | custom-call | flops 268435456 | bytes 12582912 | tf_op jit(solution)/shard_map/pallas_call | solution.py:190
  174.3 1.5 broadcast_select_fusion.refs_0_
  175.8 0.0 copy-start.1
  175.8 0.0 copy-start.4
  175.8 40.8 %shard_map.67 = f32[128,128]{1,0:T(8,128)} custom-call(f32[128,128]{1,0:T(8,128)} %broadcast_select_fusion.refs_0_, f32[128,8192]{1,0:T(8,128)} %bitcast.22), custom_call_target="tpu_custom_call" | custom-call | flops 268435456 | bytes 12582912 | tf_op jit(solution)/shard_map/pallas_call | solution.py:190
  216.6 0.0 copy-done.3
  216.6 1.5 add_subtract_fusion.refs_0_
  218.1 43.1 %shard_map.68 = f32[128,128]{1,0:T(8,128)} custom-call(f32[128,128]{1,0:T(8,128)} %add_subtract_fusion.refs_0_, f32[128,8192]{1,0:T(8,128)} %bitcast.20), custom_call_target="tpu_custom_call" | custom-call | flops 268435456 | bytes 12582912 | tf_op jit(solution)/shard_map/pallas_call | solution.py:190
  261.2 0.0 copy-done.1
  261.2 0.0 copy-done.4
  261.2 0.7 select_add_fusion
  (2 shorter events, 0.0 us)
Async XLA Ops:
  6.5 57.3 %all-gather.2.cloned.1.call-start = ((), (), s32[]{:S(2)}) async-start(), calls=%async_computation | async-start | bytes 5242880 | tf_op jit(solution)/shard_map/all_gather | solution.py:216
  79.3 5.2 %copy-start = (f32[8192,128]{1,0:T(8,128)S(1)}, f32[8192,128]{1,0:T(8,128)}, u32[]{:S(2)}) copy-start(f32[8192,128]{1,0:T(8,128)} %shard_map.64) | copy-start | bytes 12582916
  92.2 43.3 %copy-start.2 = (f32[128,128]{1,0:T(8,128)S(1)}, f32[128,128]{1,0:T(8,128)}, u32[]{:S(2)}) copy-start(f32[128,128]{1,0:T(8,128)} %refs_0_.1) | copy-start | bytes 196612
  137.0 79.7 %copy-start.3 = (f32[128,128]{1,0:T(8,128)S(1)}, f32[128,128]{1,0:T(8,128)}, u32[]{:S(2)}) copy-start(f32[128,128]{1,0:T(8,128)} %shard_map.65) | copy-start | bytes 196612
  175.8 85.4 %copy-start.1 = (f32[128,128]{1,0:T(8,128)S(1)}, f32[128,128]{1,0:T(8,128)}, u32[]{:S(2)}) copy-start(f32[128,128]{1,0:T(8,128)} %convolution_select_fusion.refs_0_) | copy-start | bytes 196612
  175.8 85.4 %copy-start.4 = (f32[128,128]{1,0:T(8,128)S(1)}, f32[128,128]{1,0:T(8,128)}, u32[]{:S(2)}) copy-start(f32[128,128]{1,0:T(8,128)} %shard_map.66) | copy-start | bytes 196612
Sparse Core Ops, SparseCore 0:
  9.2 54.5 all-gather.1
where the time goes:
time: 272 us; the launch traced here: 269 us
  Pallas kernels  210 us (77%)
  local copies, waits for them, and re-layouts  20.9 us (8%)
  between operations  15.7 us (6%)
  other arithmetic  10.7 us (4%)
  matrix products  9.85 us (4%)
    pallas_call x4, Pallas kernels, gather_product(): pl.pallas_call(functools.partial(gather_kernel, fused=True), out_shape=ja...  165 us
    pallas_call x1, Pallas kernels, gather_rows(): pl.pallas_call(functools.partial(gather_kernel, fused=False), out_shape=j...  45.1 us
    unnamed x12, local copies, waits for them, and re-layouts  10.5 us
    dot_general x1, matrix products, product(): jnp.dot(matrix, gather_rows(vector, cid), precision=lax.Precision.HIGHEST...  7.61 us
    reshape x1, local copies, waits for them, and re-layouts, masked(): block_rows.reshape(rblocks, bsz, width, bsz)  6.84 us
  transfers between devices with their start and end apart: 1, of which 1 were waited for; matrix products, arithmetic and copies ran while one was open for 3% of the time, Pallas kernels for 17%

commit v1 on v0

--- a/solution.py
+++ b/solution.py
@@ -54,7 +54,7 @@
         x_ref, f_ref, out_ref, G, acc, local_sem, send_sem, recv_z, recv_y, recv_c = refs
     else:
         x_ref, out_ref, G, local_sem, send_sem, recv_z, recv_y, recv_c = refs
-    nb = x_ref.shape[0]
+    nb, w = x_ref.shape
     r = lax.axis_index("row")
     c = lax.axis_index("col")
     y = r // (NZ * NC)
@@ -64,11 +64,11 @@
     def dev(yy, zz, kk):
         return (((yy + NY) % NY) * NZ + (zz + NZ) % NZ) * NC + kk
 
-    def slot(yy, zz, kk):
-        return kk * (NY * NZ) + ((yy + NY) % NY) * NZ + (zz + NZ) % NZ
-
-    def rows(first, n=1):
-        return G.at[pl.ds(pl.multiple_of(first * nb, nb), n * nb)]
+    def blk(yy, zz, kk):
+        return G.at[((yy + NY) % NY) * NZ + (zz + NZ) % NZ, kk]
+
+    def chunk(kk, yy, lo=0, n=NZ):
+        return G.at[pl.ds(((yy + NY) % NY) * NZ + lo, n), kk]
 
     zr, zl = dev(y, z + 1, k), dev(y, z - 1, k)
     yr, yl = dev(y + 1, z, k), dev(y - 1, z, k)
@@ -79,78 +79,68 @@
         pl.semaphore_signal(barrier, inc=1, device_id=(d, c), device_id_type=MESH)
     pl.semaphore_wait(barrier, 5)
 
-    own = slot(y, z, k)
-    local = pltpu.make_async_copy(x_ref, rows(own), local_sem.at[0])
+    local = pltpu.make_async_copy(x_ref, blk(y, z, k), local_sem.at[0])
     local.start()
     if fused:
         acc[...] = jnp.zeros_like(acc)
 
     sends = []
 
-    def remote(src, dst, si, rsem, d):
+    def remote(src, dst, rsem, d, si=0):
         return pltpu.make_async_remote_copy(
             src_ref=src, dst_ref=dst, send_sem=send_sem.at[si], recv_sem=rsem,
             device_id=(d, c), device_id_type=MESH,
         )
 
     def send(src, dst, rsem, d):
-        cp = remote(src, dst, len(sends), rsem, d)
+        cp = remote(src, dst, rsem, d, len(sends))
         cp.start()
         sends.append(cp)
 
-    def wait_z(zsrc):
-        remote(x_ref, rows(slot(y, zsrc, k)), 0, recv_z.at[(zsrc + NZ) % NZ], zr).wait_recv()
-
-    def chunk_start(kk, yy):
-        return kk * (NY * NZ) + ((yy + NY) % NY) * NZ
-
-    def chunk(kk, yy, lo=0, n=NZ):
-        return rows(chunk_start(kk, yy) + lo, n)
-
-    def multiply(kk, yy):
+    def wait(ref, rsem):
+        remote(ref, ref, rsem, partner).wait_recv()
+
+    def multiply(yy):
         if fused:
-            s0 = chunk_start(kk, yy)
-            cols = pl.ds(pl.multiple_of(s0 * nb, nb), NZ * nb)
+            plane = (yy + NY) % NY
+            cols = pl.ds(pl.multiple_of(plane * (NZ * NC * nb), nb), NZ * NC * nb)
+            vec = G[pl.ds(plane * NZ, NZ)].reshape(NZ * NC * nb, w)
             acc[...] += jnp.dot(
-                f_ref[:, cols], G[cols, :],
+                f_ref[:, cols], vec,
                 precision=lax.Precision.HIGHEST, preferred_element_type=jnp.float32,
             )
 
     for s in range(4):
         if s >= 1:
-            wait_z(z - s)
-        src = x_ref if s == 0 else rows(slot(y, z - s, k))
-        send(src, rows(slot(y, z - s, k)), recv_z.at[(z - s + NZ) % NZ], zr)
+            wait(blk(y, z - s, k), recv_z.at[(z - s + NZ) % NZ])
+        send(x_ref if s == 0 else blk(y, z - s, k), blk(y, z - s, k), recv_z.at[(z - s + NZ) % NZ], zr)
         if s < 3:
             if s >= 1:
-                wait_z(z + s)
-            src = x_ref if s == 0 else rows(slot(y, z + s, k))
-            send(src, rows(slot(y, z + s, k)), recv_z.at[(z + s) % NZ], zl)
-    wait_z(z - 4)
-    wait_z(z + 3)
+                wait(blk(y, z + s, k), recv_z.at[(z + s) % NZ])
+            send(x_ref if s == 0 else blk(y, z + s, k), blk(y, z + s, k), recv_z.at[(z + s) % NZ], zl)
+    wait(blk(y, z - 4, k), recv_z.at[(z - 4 + NZ) % NZ])
+    wait(blk(y, z + 3, k), recv_z.at[(z + 3) % NZ])
     local.wait()
 
     half = NZ // 2
     send(chunk(k, y), chunk(k, y), recv_y.at[0], yr)
     send(chunk(k, y), chunk(k, y), recv_y.at[1], yl)
     send(chunk(k, y), chunk(k, y), recv_c.at[0], partner)
-    multiply(k, y)
-    remote(chunk(k, y - 1), chunk(k, y - 1), 0, recv_y.at[0], yr).wait_recv()
+    wait(chunk(k, y - 1), recv_y.at[0])
     send(chunk(k, y - 1, 0, half), chunk(k, y - 1, 0, half), recv_y.at[2], yr)
     send(chunk(k, y - 1), chunk(k, y - 1), recv_c.at[3], partner)
-    remote(chunk(k, y + 1), chunk(k, y + 1), 0, recv_y.at[1], yl).wait_recv()
+    wait(chunk(k, y + 1), recv_y.at[1])
     send(chunk(k, y + 1, half, half), chunk(k, y + 1, half, half), recv_y.at[3], yl)
     send(chunk(k, y + 1), chunk(k, y + 1), recv_c.at[1], partner)
-    multiply(k, y - 1)
-    multiply(k, y + 1)
-    remote(chunk(k, y + 2, 0, half), chunk(k, y + 2, 0, half), 0, recv_y.at[2], yr).wait_recv()
-    remote(chunk(k, y + 2, half, half), chunk(k, y + 2, half, half), 0, recv_y.at[3], yl).wait_recv()
+    wait(chunk(1 - k, y), recv_c.at[0])
+    multiply(y)
+    wait(chunk(k, y + 2, 0, half), recv_y.at[2])
+    wait(chunk(k, y + 2, half, half), recv_y.at[3])
     send(chunk(k, y + 2), chunk(k, y + 2), recv_c.at[2], partner)
-    multiply(k, y + 2)
-
-    for d in (0, 3, 1, 2):
-        remote(chunk(1 - k, y + d), chunk(1 - k, y + d), 0, recv_c.at[d], partner).wait_recv()
-        multiply(1 - k, y + d)
+
+    for d in (3, 1, 2):
+        wait(chunk(1 - k, y + d), recv_c.at[d])
+        multiply(y + d)
 
     for cp in sends:
         cp.wait_send()
@@ -172,39 +162,34 @@
 
 def gather_rows(x, cid):
     nb, w = x.shape
-    n = NY * NZ * NC
+    shape = (NY * NZ, NC, nb, w)
     return pl.pallas_call(
         functools.partial(gather_kernel, fused=False),
-        out_shape=jax.ShapeDtypeStruct((n * nb, w), x.dtype),
+        out_shape=jax.ShapeDtypeStruct(shape, x.dtype),
         in_specs=[pl.BlockSpec(memory_space=pltpu.VMEM)],
         out_specs=pl.BlockSpec(memory_space=pltpu.VMEM),
-        scratch_shapes=[pltpu.VMEM((n * nb, w), x.dtype)] + _sems(),
+        scratch_shapes=[pltpu.VMEM(shape, x.dtype)] + _sems(),
         compiler_params=pltpu.CompilerParams(collective_id=cid, has_side_effects=True),
-        cost_estimate=pl.CostEstimate(flops=0, transcendentals=0, bytes_accessed=2 * n * nb * w * 4),
-    )(x)
+        cost_estimate=pl.CostEstimate(flops=0, transcendentals=0, bytes_accessed=2 * x.size * 64 * 4),
+    )(x).reshape(-1, w)
 
 
 def gather_product(matrix, x, cid):
     nb, w = x.shape
-    n = NY * NZ * NC
+    shape = (NY * NZ, NC, nb, w)
     return pl.pallas_call(
         functools.partial(gather_kernel, fused=True),
         out_shape=jax.ShapeDtypeStruct((matrix.shape[0], w), jnp.float32),
         in_specs=[pl.BlockSpec(memory_space=pltpu.VMEM)] * 2,
         out_specs=pl.BlockSpec(memory_space=pltpu.VMEM),
-        scratch_shapes=[pltpu.VMEM((n * nb, w), x.dtype), pltpu.VMEM((matrix.shape[0], w), jnp.float32)]
+        scratch_shapes=[pltpu.VMEM(shape, x.dtype), pltpu.VMEM((matrix.shape[0], w), jnp.float32)]
         + _sems(),
         compiler_params=pltpu.CompilerParams(collective_id=cid, has_side_effects=True),
         cost_estimate=pl.CostEstimate(
             flops=2 * matrix.shape[0] * matrix.shape[1] * w, transcendentals=0,
-            bytes_accessed=(matrix.size + 2 * n * nb * w) * 4,
+            bytes_accessed=(matrix.size + 2 * x.size * 64) * 4,
         ),
     )(x, matrix)
-
-
-def to_slot_order(cols):
-    rows = cols.shape[0]
-    return cols.reshape(rows, NY * NZ, NC, B).transpose(0, 2, 1, 3).reshape(rows, -1)
 
 
 def body(factor, rhs, parent, bounds, slot, structure):
@@ -214,8 +199,8 @@
     same_mine = lax.dynamic_slice_in_dim(same, first, RB, 0)
     link_mine = lax.dynamic_slice_in_dim(link, first, RB, 0)
     full_rows = lax.all_gather(factor, "col", axis=1, tiled=True)
-    diag_part = to_slot_order(masked(full_rows, same_mine))
-    link_part = to_slot_order(masked(full_rows, link_mine))
+    diag_part = masked(full_rows, same_mine)
+    link_part = masked(full_rows, link_mine)
 
     calls = [0]
 

time: 272 us -> 251 us (0.923)
  local copies, waits for them, and re-layouts: 20.9 us -> 3.33 us
  matrix products: 9.85 us -> 5.74 us
    unnamed x12 -> x16, local copies, waits for them, and re-layouts: 10.5 us -> 0.03 us
    reshape x1 -> x0, local copies, waits for them, and re-layouts: 6.84 us -> none  [masked(): block_rows.reshape(rblocks, bsz, width, bsz)]
    dot_general x1, matrix products: 7.61 us -> 4.83 us  [product(): jnp.dot(matrix, gather_rows(vector, cid), precision=lax.Precision.HIGHEST...]
  transfers between devices with their start and end apart: 1 -> 1, of which waited for: 1 -> 1; matrix products, arithmetic and copies ran while one was open for 3% -> 3% of each run, Pallas kernels for 17% -> 18%
where the time goes in v1:
time: 251 us; the launch traced here: 250 us
  Pallas kernels  211 us (84%)
  between operations  15.3 us (6%)
  other arithmetic  11.3 us (5%)
  matrix products  5.74 us (2%)
  waiting for transfers between devices  3.92 us (2%)
  local copies, waits for them, and re-layouts  3.33 us (1%)
    pallas_call x4, Pallas kernels, gather_product(): pl.pallas_call(functools.partial(gather_kernel, fused=True), out_shape=ja...  166 us
    pallas_call x1, Pallas kernels, gather_rows(): pl.pallas_call(functools.partial(gather_kernel, fused=False), out_shape=j...  45.1 us
  transfers between devices with their start and end apart: 1, of which 1 were waited for; matrix products, arithmetic and copies ran while one was open for 3% of the time, Pallas kernels for 18%

profile of v1, /device:TPU:1, one launch (start us, length us, event | category | flops | bytes accessed | tf_op | source)
XLA Modules:
  0.0 250.4 jit_solution(9995629896439926453)
XLA Ops:
  6.5 0.0 copy-start
  6.5 0.0 copy-start.7
  6.5 0.0 all-gather.2.cloned.1.call-start
  6.5 0.7 all-gather.2.cloned.1.call-update
  7.3 0.7 slice.3
  8.0 0.7 compare_select_fusion
  8.7 1.3 gather_fusion
  10.0 0.8 select_reduce_fusion
  10.7 0.1 convert_reduce_fusion
  10.8 0.6 dynamic-slice
  11.4 0.6 dynamic_slice.9
  12.0 45.1 %shard_map.64 = f32[32,2,128,128]{3,2,1,0:T(8,128)} custom-call(f32[128,128]{1,0:T(8,128)} %refs_0_.1), custom_call_target="tpu_custom_call" | custom-call | bytes 8388608 | tf_op jit(solution)/shard_map/pallas_call | solution.py:166
  58.9 0.0 copy-done
  58.9 0.2 fusion.2
  59.1 0.0 copy-done.7
  59.1 0.2 fusion.3
  59.3 0.3 fusion.1
  59.6 0.2 fusion
  59.9 0.7 fusion.15
  60.5 0.1 broadcast_bitcast_fusion
  60.6 3.2 %all-gather.2.cloned.1.call-done = f32[128,8192]{1,0:T(8,128)} async-done(((f32[128,2048]{1,0:T(8,128)}), f32[128,8192]{1,0:T(8,128)}) %all-gather.2.cloned.1.call-update) | async-done | bytes 4194320 | tf_op jit(solution)/shard_map/all_gather | solution.py:201
  63.8 0.0 copy-start.2
  63.8 4.9 %broadcast_multiply_fusion = (f32[128,8192]{1,0:T(8,128)}, f32[128,8192]{1,0:T(8,128)S(1)}) fusion(f32[128,8192]{1,0:T(8,128)} %all-gather.2.cloned.1.call-done, f32[8192]{0:T(1024)S(1)} %get-tuple-element.7, f32[8192]{0:T(1024)S(1)} %get-tuple-element.8), kind=kLoop, calls=%fused_computation.1 | loop fusion | flops 2097152 | bytes 12648448 | tf_op jit(solution)/shard_map/mul | solution.py:46
  68.7 0.0 copy-start.1
  68.7 0.0 copy-done.2
  68.7 4.8 %convolution_select_fusion.refs_0_ = f32[128,128]{1,0:T(8,128)} fusion(f32[128,8192]{1,0:T(8,128)S(1)} %get-tuple-element.6.refs_1_, f32[8192,128]{1,0:T(8,128)S(1)} %bitcast.16, pred[]{:T(512)} %bitcast), kind=kOutput, calls=%fused_computation.3 | convolution fusion | flops 1610629120 | bytes 8454145 | tf_op jit(solution)/shard_map/dot_general | solution.py:211
  73.5 0.0 copy-done.1
  73.5 0.0 copy-start.4
  73.5 43.7 %shard_map.65 = f32[128,128]{1,0:T(8,128)} custom-call(f32[128,128]{1,0:T(8,128)} %convolution_select_fusion.refs_0_, f32[128,8192]{1,0:T(8,128)} %get-tuple-element.5.refs_1_), custom_call_target="tpu_custom_call" | custom-call | flops 268435456 | bytes 12582912 | tf_op jit(solution)/shard_map/pallas_call | solution.py:180
  117.2 0.0 copy-done.4
  117.3 1.5 sub.6.refs_0_
  118.7 0.0 copy-start.5
  118.7 37.6 %shard_map.66 = f32[128,128]{1,0:T(8,128)} custom-call(f32[128,128]{1,0:T(8,128)} %sub.6.refs_0_, f32[128,8192]{1,0:T(8,128)} %copy-done.1), custom_call_target="tpu_custom_call" | custom-call | flops 268435456 | bytes 12582912 | tf_op jit(solution)/shard_map/pallas_call | solution.py:180
  156.3 0.6 broadcast_select_fusion.refs_0_
  157.0 0.0 copy-start.3
  157.0 0.0 copy-start.6
  157.0 41.6 %shard_map.67 = f32[128,128]{1,0:T(8,128)} custom-call(f32[128,128]{1,0:T(8,128)} %broadcast_select_fusion.refs_0_, f32[128,8192]{1,0:T(8,128)} %get-tuple-element.5.refs_1_), custom_call_target="tpu_custom_call" | custom-call | flops 268435456 | bytes 12582912 | tf_op jit(solution)/shard_map/pallas_call | solution.py:180
  198.6 0.0 copy-done.5
  198.6 1.5 add_subtract_fusion.refs_0_
  200.1 42.8 %shard_map.68 = f32[128,128]{1,0:T(8,128)} custom-call(f32[128,128]{1,0:T(8,128)} %add_subtract_fusion.refs_0_, f32[128,8192]{1,0:T(8,128)} %copy-done.1), custom_call_target="tpu_custom_call" | custom-call | flops 268435456 | bytes 12582912 | tf_op jit(solution)/shard_map/pallas_call | solution.py:180
  242.9 0.0 copy-done.3
  242.9 0.0 copy-done.6
  242.9 0.7 select_add_fusion
  (3 shorter events, 0.0 us)
Async XLA Ops:
  6.5 52.4 %copy-start = (s32[7]{0:T(128)S(1)}, s32[7]{0:T(128)}, u32[]{:S(2)}) copy-start(s32[7]{0:T(128)} %param.8) | copy-start | bytes 88
  6.5 52.6 %copy-start.7 = (s32[7,64]{1,0:T(8,128)S(1)}, s32[7,64]{1,0:T(8,128)}, u32[]{:S(2)}) copy-start(s32[7,64]{1,0:T(8,128)} %param.11) | copy-start | bytes 5380
  6.5 57.3 %all-gather.2.cloned.1.call-start = ((), (), s32[]{:S(2)}) async-start(), calls=%async_computation | async-start | bytes 5242880 | tf_op jit(solution)/shard_map/all_gather | solution.py:201
  63.8 4.9 %copy-start.2 = (f32[32,2,128,128]{3,2,1,0:T(8,128)S(1)}, f32[32,2,128,128]{3,2,1,0:T(8,128)}, u32[]{:S(2)}) copy-start(f32[32,2,128,128]{3,2,1,0:T(8,128)} %shard_map.64) | copy-start | bytes 12582916
  68.7 4.8 %copy-start.1 = (f32[128,8192]{1,0:T(8,128)}, f32[128,8192]{1,0:T(8,128)S(1)}, u32[]{:S(2)}) copy-start(f32[128,8192]{1,0:T(8,128)S(1)} %get-tuple-element.6.refs_1_) | copy-start | bytes 12582916
  73.5 43.7 %copy-start.4 = (f32[128,128]{1,0:T(8,128)S(1)}, f32[128,128]{1,0:T(8,128)}, u32[]{:S(2)}) copy-start(f32[128,128]{1,0:T(8,128)} %refs_0_.1) | copy-start | bytes 196612
  118.7 79.9 %copy-start.5 = (f32[128,128]{1,0:T(8,128)S(1)}, f32[128,128]{1,0:T(8,128)}, u32[]{:S(2)}) copy-start(f32[128,128]{1,0:T(8,128)} %shard_map.65) | copy-start | bytes 196612
  157.0 85.9 %copy-start.3 = (f32[128,128]{1,0:T(8,128)S(1)}, f32[128,128]{1,0:T(8,128)}, u32[]{:S(2)}) copy-start(f32[128,128]{1,0:T(8,128)} %convolution_select_fusion.refs_0_) | copy-start | bytes 196612
  157.0 85.9 %copy-start.6 = (f32[128,128]{1,0:T(8,128)S(1)}, f32[128,128]{1,0:T(8,128)}, u32[]{:S(2)}) copy-start(f32[128,128]{1,0:T(8,128)} %shard_map.66) | copy-start | bytes 196612
Sparse Core Ops, SparseCore 0:
  9.2 54.5 all-gather.1

commit v2 on v1

--- a/solution.py
+++ b/solution.py
@@ -110,6 +110,16 @@
                 precision=lax.Precision.HIGHEST, preferred_element_type=jnp.float32,
             )
 
+    offs = [0, -1, 1, -2, 2, -3, 3, -4]
+    to_right = {0, -1, -2, -3}
+
+    def spread(off):
+        i = offs.index(off)
+        ref = x_ref if off == 0 else blk(y, z + off, k)
+        send(ref, blk(y, z + off, k), recv_y.at[0, i], yr)
+        send(ref, blk(y, z + off, k), recv_y.at[1, i], yl)
+        send(ref, blk(y, z + off, k), recv_c.at[0, i], partner)
+
     for s in range(4):
         if s >= 1:
             wait(blk(y, z - s, k), recv_z.at[(z - s + NZ) % NZ])
@@ -118,29 +128,39 @@
             if s >= 1:
                 wait(blk(y, z + s, k), recv_z.at[(z + s) % NZ])
             send(x_ref if s == 0 else blk(y, z + s, k), blk(y, z + s, k), recv_z.at[(z + s) % NZ], zl)
+        if s == 0:
+            spread(0)
+        else:
+            spread(-s)
+            if s < 3:
+                spread(s)
     wait(blk(y, z - 4, k), recv_z.at[(z - 4 + NZ) % NZ])
+    spread(-4)
     wait(blk(y, z + 3, k), recv_z.at[(z + 3) % NZ])
+    spread(3)
     local.wait()
 
-    half = NZ // 2
-    send(chunk(k, y), chunk(k, y), recv_y.at[0], yr)
-    send(chunk(k, y), chunk(k, y), recv_y.at[1], yl)
-    send(chunk(k, y), chunk(k, y), recv_c.at[0], partner)
-    wait(chunk(k, y - 1), recv_y.at[0])
-    send(chunk(k, y - 1, 0, half), chunk(k, y - 1, 0, half), recv_y.at[2], yr)
-    send(chunk(k, y - 1), chunk(k, y - 1), recv_c.at[3], partner)
-    wait(chunk(k, y + 1), recv_y.at[1])
-    send(chunk(k, y + 1, half, half), chunk(k, y + 1, half, half), recv_y.at[3], yl)
-    send(chunk(k, y + 1), chunk(k, y + 1), recv_c.at[1], partner)
-    wait(chunk(1 - k, y), recv_c.at[0])
-    multiply(y)
-    wait(chunk(k, y + 2, 0, half), recv_y.at[2])
-    wait(chunk(k, y + 2, half, half), recv_y.at[3])
-    send(chunk(k, y + 2), chunk(k, y + 2), recv_c.at[2], partner)
-
-    for d in (3, 1, 2):
-        wait(chunk(1 - k, y + d), recv_c.at[d])
+    for i, off in enumerate(offs):
+        wait(blk(y - 1, z + off, k), recv_y.at[0, i])
+        if off in to_right:
+            send(blk(y - 1, z + off, k), blk(y - 1, z + off, k), recv_y.at[2, i], yr)
+        send(blk(y - 1, z + off, k), blk(y - 1, z + off, k), recv_c.at[3, i], partner)
+        wait(blk(y + 1, z + off, k), recv_y.at[1, i])
+        if off not in to_right:
+            send(blk(y + 1, z + off, k), blk(y + 1, z + off, k), recv_y.at[3, i], yl)
+        send(blk(y + 1, z + off, k), blk(y + 1, z + off, k), recv_c.at[1, i], partner)
+
+    def partner_plane(d):
+        for i, off in enumerate(offs):
+            wait(blk(y + d, z + off, 1 - k), recv_c.at[d % NY, i])
         multiply(y + d)
+
+    partner_plane(0)
+    for i, off in enumerate(offs):
+        wait(blk(y + 2, z + off, k), recv_y.at[2 if off in to_right else 3, i])
+        send(blk(y + 2, z + off, k), blk(y + 2, z + off, k), recv_c.at[2, i], partner)
+    for d in (-1, 1, 2):
+        partner_plane(d)
 
     for cp in sends:
         cp.wait_send()
@@ -153,10 +173,10 @@
 def _sems():
     return [
         pltpu.SemaphoreType.DMA((1,)),
-        pltpu.SemaphoreType.DMA((16,)),
+        pltpu.SemaphoreType.DMA((64,)),
         pltpu.SemaphoreType.DMA((NZ,)),
-        pltpu.SemaphoreType.DMA((4,)),
-        pltpu.SemaphoreType.DMA((4,)),
+        pltpu.SemaphoreType.DMA((4, NZ)),
+        pltpu.SemaphoreType.DMA((NY, NZ)),
     ]
 
 

time: 251 us -> 219 us (0.87)
  Pallas kernels: 211 us -> 170 us
  waiting for transfers between devices: 3.92 us -> 11.6 us
    pallas_call x4, Pallas kernels: 166 us -> 133 us  [gather_product(): pl.pallas_call(functools.partial(gather_kernel, fused=True), out_shape=ja...]
    all_gather x1, waiting for transfers between devices: 3.21 us -> 10.8 us  [body(): full_rows = lax.all_gather(factor, 'col', axis=1, tiled=True)]
    pallas_call x1, Pallas kernels: 45.1 us -> 37.4 us  [gather_rows(): pl.pallas_call(functools.partial(gather_kernel, fused=False), out_shape=j...]
  transfers between devices with their start and end apart: 1 -> 1, of which waited for: 1 -> 1; matrix products, arithmetic and copies ran while one was open for 3% -> 3% of each run, Pallas kernels for 18% -> 17%
where the time goes in v2:
time: 219 us; the launch traced here: 218 us
  Pallas kernels  170 us (78%)
  between operations  15.3 us (7%)
  other arithmetic  12.1 us (6%)
  waiting for transfers between devices  11.6 us (5%)
  matrix products  5.74 us (3%)
  local copies, waits for them, and re-layouts  3.33 us (2%)
    pallas_call x4, Pallas kernels, gather_product(): pl.pallas_call(functools.partial(gather_kernel, fused=True), out_shape=ja...  133 us
    pallas_call x1, Pallas kernels, gather_rows(): pl.pallas_call(functools.partial(gather_kernel, fused=False), out_shape=j...  37.4 us
    all_gather x1, waiting for transfers between devices, body(): full_rows = lax.all_gather(factor, 'col', axis=1, tiled=True)  10.8 us
    mul x1, other arithmetic, masked(): block_rows.reshape(rblocks, bsz, width, bsz)  4.86 us
    dot_general x1, matrix products, product(): jnp.dot(matrix, gather_rows(vector, cid), precision=lax.Precision.HIGHEST...  4.83 us
  transfers between devices with their start and end apart: 1, of which 1 were waited for; matrix products, arithmetic and copies ran while one was open for 3% of the time, Pallas kernels for 17%

profile of v2, /device:TPU:1, one launch (start us, length us, event | category | flops | bytes accessed | tf_op | source)
XLA Modules:
  0.0 218.3 jit_solution(352240266466652955)
XLA Ops:
  6.5 0.0 copy-start
  6.5 0.0 copy-start.7
  6.5 0.0 all-gather.2.cloned.1.call-start
  6.5 0.7 all-gather.2.cloned.1.call-update
  7.3 0.7 slice.3
  8.0 0.7 compare_select_fusion
  8.7 1.3 gather_fusion
  10.0 0.8 select_reduce_fusion
  10.7 0.1 convert_reduce_fusion
  10.8 0.6 dynamic-slice
  11.4 0.6 dynamic_slice.9
  12.0 37.4 %shard_map.64 = f32[32,2,128,128]{3,2,1,0:T(8,128)} custom-call(f32[128,128]{1,0:T(8,128)} %refs_0_.1), custom_call_target="tpu_custom_call" | custom-call | bytes 8388608 | tf_op jit(solution)/shard_map/pallas_call | solution.py:186
  51.3 0.0 copy-done
  51.3 0.2 fusion.2
  51.5 0.0 copy-done.7
  51.5 0.2 fusion.3
  51.7 0.3 fusion.1
  52.0 0.2 fusion
  52.2 0.7 fusion.15
  52.9 0.1 broadcast_bitcast_fusion
  53.0 10.8 %all-gather.2.cloned.1.call-done = f32[128,8192]{1,0:T(8,128)} async-done(((f32[128,2048]{1,0:T(8,128)}), f32[128,8192]{1,0:T(8,128)}) %all-gather.2.cloned.1.call-update) | async-done | bytes 4194320 | tf_op jit(solution)/shard_map/all_gather | solution.py:221
  63.8 0.0 copy-start.2
  63.8 4.9 %broadcast_multiply_fusion = (f32[128,8192]{1,0:T(8,128)}, f32[128,8192]{1,0:T(8,128)S(1)}) fusion(f32[128,8192]{1,0:T(8,128)} %all-gather.2.cloned.1.call-done, f32[8192]{0:T(1024)S(1)} %get-tuple-element.7, f32[8192]{0:T(1024)S(1)} %get-tuple-element.8), kind=kLoop, calls=%fused_computation.1 | loop fusion | flops 2097152 | bytes 12648448 | tf_op jit(solution)/shard_map/mul | solution.py:46
  68.7 0.0 copy-start.1
  68.7 0.0 copy-done.2
  68.7 4.8 %convolution_select_fusion.refs_0_ = f32[128,128]{1,0:T(8,128)} fusion(f32[128,8192]{1,0:T(8,128)S(1)} %get-tuple-element.6.refs_1_, f32[8192,128]{1,0:T(8,128)S(1)} %bitcast.16, pred[]{:T(512)} %bitcast), kind=kOutput, calls=%fused_computation.3 | convolution fusion | flops 1610629120 | bytes 8454145 | tf_op jit(solution)/shard_map/dot_general | solution.py:231
  73.5 0.0 copy-done.1
  73.5 0.0 copy-start.4
  73.5 35.1 %shard_map.65 = f32[128,128]{1,0:T(8,128)} custom-call(f32[128,128]{1,0:T(8,128)} %convolution_select_fusion.refs_0_, f32[128,8192]{1,0:T(8,128)} %get-tuple-element.5.refs_1_), custom_call_target="tpu_custom_call" | custom-call | flops 268435456 | bytes 12582912 | tf_op jit(solution)/shard_map/pallas_call | solution.py:200
  108.6 0.0 copy-done.4
  108.6 1.5 sub.6.refs_0_
  110.1 0.0 copy-start.5
  110.1 31.5 %shard_map.66 = f32[128,128]{1,0:T(8,128)} custom-call(f32[128,128]{1,0:T(8,128)} %sub.6.refs_0_, f32[128,8192]{1,0:T(8,128)} %copy-done.1), custom_call_target="tpu_custom_call" | custom-call | flops 268435456 | bytes 12582912 | tf_op jit(solution)/shard_map/pallas_call | solution.py:200
  141.6 1.5 broadcast_select_fusion.refs_0_
  143.1 0.0 copy-start.3
  143.1 0.0 copy-start.6
  143.1 32.7 %shard_map.67 = f32[128,128]{1,0:T(8,128)} custom-call(f32[128,128]{1,0:T(8,128)} %broadcast_select_fusion.refs_0_, f32[128,8192]{1,0:T(8,128)} %get-tuple-element.5.refs_1_), custom_call_target="tpu_custom_call" | custom-call | flops 268435456 | bytes 12582912 | tf_op jit(solution)/shard_map/pallas_call | solution.py:200
  175.8 0.0 copy-done.5
  175.8 1.5 add_subtract_fusion.refs_0_
  177.3 33.5 %shard_map.68 = f32[128,128]{1,0:T(8,128)} custom-call(f32[128,128]{1,0:T(8,128)} %add_subtract_fusion.refs_0_, f32[128,8192]{1,0:T(8,128)} %copy-done.1), custom_call_target="tpu_custom_call" | custom-call | flops 268435456 | bytes 12582912 | tf_op jit(solution)/shard_map/pallas_call | solution.py:200
  210.8 0.0 copy-done.3
  210.8 0.0 copy-done.6
  210.8 0.7 select_add_fusion
  (3 shorter events, 0.0 us)
Async XLA Ops:
  6.5 44.7 %copy-start = (s32[7]{0:T(128)S(1)}, s32[7]{0:T(128)}, u32[]{:S(2)}) copy-start(s32[7]{0:T(128)} %param.8) | copy-start | bytes 88
  6.5 44.9 %copy-start.7 = (s32[7,64]{1,0:T(8,128)S(1)}, s32[7,64]{1,0:T(8,128)}, u32[]{:S(2)}) copy-start(s32[7,64]{1,0:T(8,128)} %param.11) | copy-start | bytes 5380
  6.5 57.3 %all-gather.2.cloned.1.call-start = ((), (), s32[]{:S(2)}) async-start(), calls=%async_computation | async-start | bytes 5242880 | tf_op jit(solution)/shard_map/all_gather | solution.py:221
  63.8 4.9 %copy-start.2 = (f32[32,2,128,128]{3,2,1,0:T(8,128)S(1)}, f32[32,2,128,128]{3,2,1,0:T(8,128)}, u32[]{:S(2)}) copy-start(f32[32,2,128,128]{3,2,1,0:T(8,128)} %shard_map.64) | copy-start | bytes 12582916
  68.7 4.8 %copy-start.1 = (f32[128,8192]{1,0:T(8,128)}, f32[128,8192]{1,0:T(8,128)S(1)}, u32[]{:S(2)}) copy-start(f32[128,8192]{1,0:T(8,128)S(1)} %get-tuple-element.6.refs_1_) | copy-start | bytes 12582916
  73.5 35.1 %copy-start.4 = (f32[128,128]{1,0:T(8,128)S(1)}, f32[128,128]{1,0:T(8,128)}, u32[]{:S(2)}) copy-start(f32[128,128]{1,0:T(8,128)} %refs_0_.1) | copy-start | bytes 196612
  110.1 65.8 %copy-start.5 = (f32[128,128]{1,0:T(8,128)S(1)}, f32[128,128]{1,0:T(8,128)}, u32[]{:S(2)}) copy-start(f32[128,128]{1,0:T(8,128)} %shard_map.65) | copy-start | bytes 196612
  143.1 67.8 %copy-start.3 = (f32[128,128]{1,0:T(8,128)S(1)}, f32[128,128]{1,0:T(8,128)}, u32[]{:S(2)}) copy-start(f32[128,128]{1,0:T(8,128)} %convolution_select_fusion.refs_0_) | copy-start | bytes 196612
  143.1 67.8 %copy-start.6 = (f32[128,128]{1,0:T(8,128)S(1)}, f32[128,128]{1,0:T(8,128)}, u32[]{:S(2)}) copy-start(f32[128,128]{1,0:T(8,128)} %shard_map.66) | copy-start | bytes 196612
Sparse Core Ops, SparseCore 0:
  9.2 54.5 all-gather.1

commit v3 on v2

--- a/solution.py
+++ b/solution.py
@@ -75,9 +75,10 @@
     partner = dev(y, z, 1 - k)
 
     barrier = pltpu.get_barrier_semaphore()
-    for d in (zr, zl, yr, yl, partner):
+    peers = (zr, zl, dev(y, z + 2, k), dev(y, z - 2, k), yr, yl, partner)
+    for d in peers:
         pl.semaphore_signal(barrier, inc=1, device_id=(d, c), device_id_type=MESH)
-    pl.semaphore_wait(barrier, 5)
+    pl.semaphore_wait(barrier, len(peers))
 
     local = pltpu.make_async_copy(x_ref, blk(y, z, k), local_sem.at[0])
     local.start()
@@ -120,24 +121,25 @@
         send(ref, blk(y, z + off, k), recv_y.at[1, i], yl)
         send(ref, blk(y, z + off, k), recv_c.at[0, i], partner)
 
-    for s in range(4):
-        if s >= 1:
-            wait(blk(y, z - s, k), recv_z.at[(z - s + NZ) % NZ])
-        send(x_ref if s == 0 else blk(y, z - s, k), blk(y, z - s, k), recv_z.at[(z - s + NZ) % NZ], zr)
-        if s < 3:
-            if s >= 1:
-                wait(blk(y, z + s, k), recv_z.at[(z + s) % NZ])
-            send(x_ref if s == 0 else blk(y, z + s, k), blk(y, z + s, k), recv_z.at[(z + s) % NZ], zl)
-        if s == 0:
-            spread(0)
-        else:
-            spread(-s)
-            if s < 3:
-                spread(s)
-    wait(blk(y, z - 4, k), recv_z.at[(z - 4 + NZ) % NZ])
-    spread(-4)
-    wait(blk(y, z + 3, k), recv_z.at[(z + 3) % NZ])
-    spread(3)
+    def recv_of(zsrc):
+        return recv_z.at[(zsrc + NZ) % NZ]
+
+    for d in (1, 2, -1, -2):
+        send(x_ref, blk(y, z, k), recv_of(z), dev(y, z + d, k))
+    spread(0)
+    wait(blk(y, z - 2, k), recv_of(z - 2))
+    send(blk(y, z - 2, k), blk(y, z - 2, k), recv_of(z - 2), dev(y, z + 1, k))
+    send(blk(y, z - 2, k), blk(y, z - 2, k), recv_of(z - 2), dev(y, z + 2, k))
+    wait(blk(y, z + 2, k), recv_of(z + 2))
+    send(blk(y, z + 2, k), blk(y, z + 2, k), recv_of(z + 2), dev(y, z - 1, k))
+    for off in (-1, 1):
+        wait(blk(y, z + off, k), recv_of(z + off))
+        spread(off)
+    spread(-2)
+    spread(2)
+    for off in (-3, 3, -4):
+        wait(blk(y, z + off, k), recv_of(z + off))
+        spread(off)
     local.wait()
 
     for i, off in enumerate(offs):

time: 219 us -> 218 us (level)
  no operation moved by 1% of the time
where the time goes in v3:
time: 218 us; the launch traced here: 217 us
  Pallas kernels  169 us (78%)
  between operations  15.3 us (7%)
  waiting for transfers between devices  12.4 us (6%)
  other arithmetic  12.1 us (6%)
  matrix products  5.74 us (3%)
  local copies, waits for them, and re-layouts  3.33 us (2%)
    pallas_call x4, Pallas kernels, gather_product(): pl.pallas_call(functools.partial(gather_kernel, fused=True), out_shape=ja...  132 us
    pallas_call x1, Pallas kernels, gather_rows(): pl.pallas_call(functools.partial(gather_kernel, fused=False), out_shape=j...  36.6 us
    all_gather x1, waiting for transfers between devices, body(): full_rows = lax.all_gather(factor, 'col', axis=1, tiled=True)  11.7 us
    mul x1, other arithmetic, masked(): block_rows.reshape(rblocks, bsz, width, bsz)  4.86 us
    dot_general x1, matrix products, product(): jnp.dot(matrix, gather_rows(vector, cid), precision=lax.Precision.HIGHEST...  4.83 us
  transfers between devices with their start and end apart: 1, of which 1 were waited for; matrix products, arithmetic and copies ran while one was open for 3% of the time, Pallas kernels for 17%

profile of v3, /device:TPU:1, one launch (start us, length us, event | category | flops | bytes accessed | tf_op | source)
XLA Modules:
  0.0 217.4 jit_solution(9010362674742954646)
XLA Ops:
  6.5 0.0 copy-start
  6.5 0.0 copy-start.7
  6.5 0.0 all-gather.2.cloned.1.call-start
  6.5 0.7 all-gather.2.cloned.1.call-update
  7.3 0.7 slice.3
  8.0 0.7 compare_select_fusion
  8.7 1.3 gather_fusion
  10.0 0.8 select_reduce_fusion
  10.7 0.1 convert_reduce_fusion
  10.8 0.6 dynamic-slice
  11.4 0.6 dynamic_slice.9
  12.0 36.6 %shard_map.64 = f32[32,2,128,128]{3,2,1,0:T(8,128)} custom-call(f32[128,128]{1,0:T(8,128)} %refs_0_.1), custom_call_target="tpu_custom_call" | custom-call | bytes 8388608 | tf_op jit(solution)/shard_map/pallas_call | solution.py:188
  50.5 0.0 copy-done
  50.5 0.2 fusion.2
  50.7 0.0 copy-done.7
  50.7 0.2 fusion.3
  50.9 0.3 fusion.1
  51.2 0.2 fusion
  51.4 0.7 fusion.15
  52.1 0.1 broadcast_bitcast_fusion
  52.2 11.7 %all-gather.2.cloned.1.call-done = f32[128,8192]{1,0:T(8,128)} async-done(((f32[128,2048]{1,0:T(8,128)}), f32[128,8192]{1,0:T(8,128)}) %all-gather.2.cloned.1.call-update) | async-done | bytes 4194320 | tf_op jit(solution)/shard_map/all_gather | solution.py:223
  63.8 0.0 copy-start.2
  63.8 4.9 %broadcast_multiply_fusion = (f32[128,8192]{1,0:T(8,128)}, f32[128,8192]{1,0:T(8,128)S(1)}) fusion(f32[128,8192]{1,0:T(8,128)} %all-gather.2.cloned.1.call-done, f32[8192]{0:T(1024)S(1)} %get-tuple-element.7, f32[8192]{0:T(1024)S(1)} %get-tuple-element.8), kind=kLoop, calls=%fused_computation.1 | loop fusion | flops 2097152 | bytes 12648448 | tf_op jit(solution)/shard_map/mul | solution.py:46
  68.7 0.0 copy-start.1
  68.7 0.0 copy-done.2
  68.7 4.8 %convolution_select_fusion.refs_0_ = f32[128,128]{1,0:T(8,128)} fusion(f32[128,8192]{1,0:T(8,128)S(1)} %get-tuple-element.6.refs_1_, f32[8192,128]{1,0:T(8,128)S(1)} %bitcast.16, pred[]{:T(512)} %bitcast), kind=kOutput, calls=%fused_computation.3 | convolution fusion | flops 1610629120 | bytes 8454145 | tf_op jit(solution)/shard_map/dot_general | solution.py:233
  73.5 0.0 copy-done.1
  73.5 0.0 copy-start.4
  73.5 35.1 %shard_map.65 = f32[128,128]{1,0:T(8,128)} custom-call(f32[128,128]{1,0:T(8,128)} %convolution_select_fusion.refs_0_, f32[128,8192]{1,0:T(8,128)} %get-tuple-element.5.refs_1_), custom_call_target="tpu_custom_call" | custom-call | flops 268435456 | bytes 12582912 | tf_op jit(solution)/shard_map/pallas_call | solution.py:202
  108.6 0.0 copy-done.4
  108.7 1.5 sub.6.refs_0_
  110.1 0.0 copy-start.5
  110.1 33.0 %shard_map.66 = f32[128,128]{1,0:T(8,128)} custom-call(f32[128,128]{1,0:T(8,128)} %sub.6.refs_0_, f32[128,8192]{1,0:T(8,128)} %copy-done.1), custom_call_target="tpu_custom_call" | custom-call | flops 268435456 | bytes 12582912 | tf_op jit(solution)/shard_map/pallas_call | solution.py:202
  143.1 1.5 broadcast_select_fusion.refs_0_
  144.6 0.0 copy-start.3
  144.6 0.0 copy-start.6
  144.6 31.8 %shard_map.67 = f32[128,128]{1,0:T(8,128)} custom-call(f32[128,128]{1,0:T(8,128)} %broadcast_select_fusion.refs_0_, f32[128,8192]{1,0:T(8,128)} %get-tuple-element.5.refs_1_), custom_call_target="tpu_custom_call" | custom-call | flops 268435456 | bytes 12582912 | tf_op jit(solution)/shard_map/pallas_call | solution.py:202
  176.4 0.0 copy-done.5
  176.4 1.5 add_subtract_fusion.refs_0_
  177.8 32.0 %shard_map.68 = f32[128,128]{1,0:T(8,128)} custom-call(f32[128,128]{1,0:T(8,128)} %add_subtract_fusion.refs_0_, f32[128,8192]{1,0:T(8,128)} %copy-done.1), custom_call_target="tpu_custom_call" | custom-call | flops 268435456 | bytes 12582912 | tf_op jit(solution)/shard_map/pallas_call | solution.py:202
  209.9 0.0 copy-done.3
  209.9 0.0 copy-done.6
  209.9 0.7 select_add_fusion
  (3 shorter events, 0.0 us)
Async XLA Ops:
  6.5 43.9 %copy-start = (s32[7]{0:T(128)S(1)}, s32[7]{0:T(128)}, u32[]{:S(2)}) copy-start(s32[7]{0:T(128)} %param.8) | copy-start | bytes 88
  6.5 44.1 %copy-start.7 = (s32[7,64]{1,0:T(8,128)S(1)}, s32[7,64]{1,0:T(8,128)}, u32[]{:S(2)}) copy-start(s32[7,64]{1,0:T(8,128)} %param.11) | copy-start | bytes 5380
  6.5 57.3 %all-gather.2.cloned.1.call-start = ((), (), s32[]{:S(2)}) async-start(), calls=%async_computation | async-start | bytes 5242880 | tf_op jit(solution)/shard_map/all_gather | solution.py:223
  63.8 4.9 %copy-start.2 = (f32[32,2,128,128]{3,2,1,0:T(8,128)S(1)}, f32[32,2,128,128]{3,2,1,0:T(8,128)}, u32[]{:S(2)}) copy-start(f32[32,2,128,128]{3,2,1,0:T(8,128)} %shard_map.64) | copy-start | bytes 12582916
  68.7 4.8 %copy-start.1 = (f32[128,8192]{1,0:T(8,128)}, f32[128,8192]{1,0:T(8,128)S(1)}, u32[]{:S(2)}) copy-start(f32[128,8192]{1,0:T(8,128)S(1)} %get-tuple-element.6.refs_1_) | copy-start | bytes 12582916
  73.5 35.1 %copy-start.4 = (f32[128,128]{1,0:T(8,128)S(1)}, f32[128,128]{1,0:T(8,128)}, u32[]{:S(2)}) copy-start(f32[128,128]{1,0:T(8,128)} %refs_0_.1) | copy-start | bytes 196612
  110.1 66.2 %copy-start.5 = (f32[128,128]{1,0:T(8,128)S(1)}, f32[128,128]{1,0:T(8,128)}, u32[]{:S(2)}) copy-start(f32[128,128]{1,0:T(8,128)} %shard_map.65) | copy-start | bytes 196612
  144.6 65.3 %copy-start.3 = (f32[128,128]{1,0:T(8,128)S(1)}, f32[128,128]{1,0:T(8,128)}, u32[]{:S(2)}) copy-start(f32[128,128]{1,0:T(8,128)} %convolution_select_fusion.refs_0_) | copy-start | bytes 196612
  144.6 65.3 %copy-start.6 = (f32[128,128]{1,0:T(8,128)S(1)}, f32[128,128]{1,0:T(8,128)}, u32[]{:S(2)}) copy-start(f32[128,128]{1,0:T(8,128)} %shard_map.66) | copy-start | bytes 196612
Sparse Core Ops, SparseCore 0:
  9.2 54.5 all-gather.1

commit v4 on v3

--- a/solution.py
+++ b/solution.py
@@ -49,11 +49,13 @@
     return shaped.reshape(block_rows.shape)
 
 
-def gather_kernel(*refs, fused):
-    if fused:
-        x_ref, f_ref, out_ref, G, acc, local_sem, send_sem, recv_z, recv_y, recv_c = refs
+def gather_kernel(*refs, mode):
+    fused = True
+    if mode == "first":
+        x_ref, floc_ref, m_ref, out_ref, fout_ref, G, f_ref, acc, local_sem, send_sem, recv_z, recv_y, recv_c, \
+            recv_x = refs
     else:
-        x_ref, out_ref, G, local_sem, send_sem, recv_z, recv_y, recv_c = refs
+        x_ref, f_ref, m_ref, out_ref, G, acc, local_sem, send_sem, recv_z, recv_y, recv_c = refs
     nb, w = x_ref.shape
     r = lax.axis_index("row")
     c = lax.axis_index("col")
@@ -75,15 +77,37 @@
     partner = dev(y, z, 1 - k)
 
     barrier = pltpu.get_barrier_semaphore()
-    peers = (zr, zl, dev(y, z + 2, k), dev(y, z - 2, k), yr, yl, partner)
+    peers = [(d, c) for d in (zr, zl, dev(y, z + 2, k), dev(y, z - 2, k), yr, yl, partner)]
+    nx = 4
+    xr, xl = (r, (c + 1) % nx), (r, (c + nx - 1) % nx)
+    if mode == "first":
+        peers += [xr, xl]
     for d in peers:
-        pl.semaphore_signal(barrier, inc=1, device_id=(d, c), device_id_type=MESH)
+        pl.semaphore_signal(barrier, inc=1, device_id=d, device_id_type=MESH)
     pl.semaphore_wait(barrier, len(peers))
 
     local = pltpu.make_async_copy(x_ref, blk(y, z, k), local_sem.at[0])
     local.start()
-    if fused:
-        acc[...] = jnp.zeros_like(acc)
+    acc[...] = jnp.zeros_like(acc)
+
+    if mode == "first":
+        wcol = floc_ref.shape[1]
+        hcol = wcol // 2
+
+        def fcols(cc, lo=0, n=wcol):
+            return f_ref.at[:, pl.ds(pl.multiple_of(((cc + nx) % nx) * wcol + lo, 128), n)]
+
+        def xcopy(src, dst, si, rsem, d):
+            return pltpu.make_async_remote_copy(
+                src_ref=src, dst_ref=dst, send_sem=send_sem.at[si], recv_sem=rsem,
+                device_id=d, device_id_type=MESH,
+            )
+
+        flocal = pltpu.make_async_copy(floc_ref, fcols(c), local_sem.at[1])
+        flocal.start()
+        xsends = [xcopy(floc_ref, fcols(c), 64, recv_x.at[0], xr), xcopy(floc_ref, fcols(c), 65, recv_x.at[1], xl)]
+        for cp in xsends:
+            cp.start()
 
     sends = []
 
@@ -107,7 +131,7 @@
             cols = pl.ds(pl.multiple_of(plane * (NZ * NC * nb), nb), NZ * NC * nb)
             vec = G[pl.ds(plane * NZ, NZ)].reshape(NZ * NC * nb, w)
             acc[...] += jnp.dot(
-                f_ref[:, cols], vec,
+                f_ref[:, cols] * m_ref[:, cols], vec,
                 precision=lax.Precision.HIGHEST, preferred_element_type=jnp.float32,
             )
 
@@ -157,52 +181,88 @@
             wait(blk(y + d, z + off, 1 - k), recv_c.at[d % NY, i])
         multiply(y + d)
 
-    partner_plane(0)
+    def partner_wait(d):
+        for i, off in enumerate(offs):
+            wait(blk(y + d, z + off, 1 - k), recv_c.at[d % NY, i])
+
+    if mode == "first":
+        xcopy(floc_ref, fcols(c - 1), 0, recv_x.at[0], xr).wait_recv()
+        xsends.append(xcopy(fcols(c - 1, 0, hcol), fcols(c - 1, 0, hcol), 66, recv_x.at[2], xr))
+        xsends[-1].start()
+        xcopy(floc_ref, fcols(c + 1), 0, recv_x.at[1], xr).wait_recv()
+        xsends.append(xcopy(fcols(c + 1, hcol, hcol), fcols(c + 1, hcol, hcol), 67, recv_x.at[3], xl))
+        xsends[-1].start()
+    else:
+        partner_wait(0)
+        multiply(y)
     for i, off in enumerate(offs):
         wait(blk(y + 2, z + off, k), recv_y.at[2 if off in to_right else 3, i])
         send(blk(y + 2, z + off, k), blk(y + 2, z + off, k), recv_c.at[2, i], partner)
-    for d in (-1, 1, 2):
-        partner_plane(d)
+    if mode == "first":
+        for d in (0, -1, 1, 2):
+            partner_wait(d)
+        flocal.wait()
+        multiply(c)
+        multiply(c - 1)
+        multiply(c + 1)
+        xcopy(fcols(c + 2, 0, hcol), fcols(c + 2, 0, hcol), 0, recv_x.at[2], xr).wait_recv()
+        xcopy(fcols(c + 2, hcol, hcol), fcols(c + 2, hcol, hcol), 0, recv_x.at[3], xr).wait_recv()
+        multiply(c + 2)
+        for cp in xsends:
+            cp.wait_send()
+        fout = pltpu.make_async_copy(f_ref, fout_ref, local_sem.at[1])
+        fout.start()
+        fout.wait()
+    else:
+        for d in (-1, 1, 2):
+            partner_wait(d)
+            multiply(y + d)
 
     for cp in sends:
         cp.wait_send()
-    if fused:
-        out_ref[...] = acc[...]
-    else:
-        out_ref[...] = G[...]
+    out_ref[...] = acc[...]
 
 
 def _sems():
     return [
-        pltpu.SemaphoreType.DMA((1,)),
-        pltpu.SemaphoreType.DMA((64,)),
+        pltpu.SemaphoreType.DMA((2,)),
+        pltpu.SemaphoreType.DMA((68,)),
         pltpu.SemaphoreType.DMA((NZ,)),
         pltpu.SemaphoreType.DMA((4, NZ)),
         pltpu.SemaphoreType.DMA((NY, NZ)),
     ]
 
 
-def gather_rows(x, cid):
+def _specs(n):
+    return [pl.BlockSpec(memory_space=pltpu.VMEM)] * n
+
+
+def first_product(floc, mask_row, x, cid):
+    nb, w = x.shape
+    rows = floc.shape[0]
+    ncol = floc.shape[1] * 4
+    return pl.pallas_call(
+        functools.partial(gather_kernel, mode="first"),
+        out_shape=(jax.ShapeDtypeStruct((rows, w), jnp.float32), jax.ShapeDtypeStruct((rows, ncol), floc.dtype)),
+        in_specs=_specs(3),
+        out_specs=(pl.BlockSpec(memory_space=pltpu.VMEM), pl.BlockSpec(memory_space=pl.ANY)),
+        scratch_shapes=[pltpu.VMEM((NY * NZ, NC, nb, w), x.dtype), pltpu.VMEM((rows, ncol), floc.dtype),
+                        pltpu.VMEM((rows, w), jnp.float32)]
+        + _sems() + [pltpu.SemaphoreType.DMA((4,))],
+        compiler_params=pltpu.CompilerParams(collective_id=cid, has_side_effects=True),
+        cost_estimate=pl.CostEstimate(
+            flops=2 * rows * ncol * w, transcendentals=0, bytes_accessed=(2 * rows * ncol + 2 * x.size * 64) * 4,
+        ),
+    )(x, floc, mask_row)
+
+
+def gather_product(matrix, mask_row, x, cid):
     nb, w = x.shape
     shape = (NY * NZ, NC, nb, w)
     return pl.pallas_call(
-        functools.partial(gather_kernel, fused=False),
-        out_shape=jax.ShapeDtypeStruct(shape, x.dtype),
-        in_specs=[pl.BlockSpec(memory_space=pltpu.VMEM)],
-        out_specs=pl.BlockSpec(memory_space=pltpu.VMEM),
-        scratch_shapes=[pltpu.VMEM(shape, x.dtype)] + _sems(),
-        compiler_params=pltpu.CompilerParams(collective_id=cid, has_side_effects=True),
-        cost_estimate=pl.CostEstimate(flops=0, transcendentals=0, bytes_accessed=2 * x.size * 64 * 4),
-    )(x).reshape(-1, w)
-
-
-def gather_product(matrix, x, cid):
-    nb, w = x.shape
-    shape = (NY * NZ, NC, nb, w)
-    return pl.pallas_call(
-        functools.partial(gather_kernel, fused=True),
+        functools.partial(gather_kernel, mode="fused"),
         out_shape=jax.ShapeDtypeStruct((matrix.shape[0], w), jnp.float32),
-        in_specs=[pl.BlockSpec(memory_space=pltpu.VMEM)] * 2,
+        in_specs=_specs(3),
         out_specs=pl.BlockSpec(memory_space=pltpu.VMEM),
         scratch_shapes=[pltpu.VMEM(shape, x.dtype), pltpu.VMEM((matrix.shape[0], w), jnp.float32)]
         + _sems(),
@@ -211,43 +271,28 @@
             flops=2 * matrix.shape[0] * matrix.shape[1] * w, transcendentals=0,
             bytes_accessed=(matrix.size + 2 * x.size * 64) * 4,
         ),
-    )(x, matrix)
+    )(x, matrix, mask_row)
 
 
 def body(factor, rhs, parent, bounds, slot, structure):
     level, same, link = block_masks(parent, bounds, slot, structure)
     first = lax.axis_index("row") * RB
     level_mine = lax.dynamic_slice_in_dim(level, first, RB, 0)
-    same_mine = lax.dynamic_slice_in_dim(same, first, RB, 0)
-    link_mine = lax.dynamic_slice_in_dim(link, first, RB, 0)
-    full_rows = lax.all_gather(factor, "col", axis=1, tiled=True)
-    diag_part = masked(full_rows, same_mine)
-    link_part = masked(full_rows, link_mine)
-
-    calls = [0]
-
-    def product(matrix, vector):
-        cid = calls[0]
-        calls[0] += 1
-        if cid == 0:
-            return jnp.dot(
-                matrix,
-                gather_rows(vector, cid),
-                precision=lax.Precision.HIGHEST,
-                preferred_element_type=jnp.float32,
-            )
-        return gather_product(matrix, vector, cid)
-
-    pieces = [rhs]
-    accums = [jnp.zeros(p.shape, jnp.float32) for p in pieces]
-    results = [jnp.zeros(p.shape, jnp.float32) for p in pieces]
-    for section in range(3):
+    same_row = jnp.repeat(lax.dynamic_slice_in_dim(same, first, RB, 0).astype(jnp.float32), B, axis=1)
+    link_row = jnp.repeat(lax.dynamic_slice_in_dim(link, first, RB, 0).astype(jnp.float32), B, axis=1)
+
+    rows0 = jnp.repeat(level_mine == 0, B)[:, None]
+    first_prod, full_rows = first_product(factor, same_row, rhs, 0)
+    solved = jnp.where(rows0, first_prod, 0.0)
+    result = solved
+    accum = gather_product(full_rows, link_row, solved, 1)
+    for section in (1, 2):
         rows = jnp.repeat(level_mine == section, B)[:, None]
-        solved = jnp.where(rows, product(diag_part, pieces[0] - accums[0]), 0.0)
-        results[0] = results[0] + solved
+        solved = jnp.where(rows, gather_product(full_rows, same_row, rhs - accum, 2 * section), 0.0)
+        result = result + solved
         if section < 2:
-            accums[0] = accums[0] + product(link_part, solved)
-    return results[0]
+            accum = accum + gather_product(full_rows, link_row, solved, 2 * section + 1)
+    return result
 
 
 def solution(mesh):

time: 218 us -> 198 us (0.908)
  between operations: 15.3 us -> 2.07 us
  waiting for transfers between devices: 12.4 us -> 0 us
  Pallas kernels: 169 us -> 181 us
  other arithmetic: 12.1 us -> 7.95 us
  matrix products: 5.74 us -> 2.25 us
    pallas_call x5, Pallas kernels: 169 us -> 181 us  [the longest x4 132 us: gather_product(): pl.pallas_call(functools.partial(gather_kernel, mode='fused'), out_shape=...]
    all_gather x1 -> x0, waiting for transfers between devices: 11.7 us -> none  [body(): full_rows = lax.all_gather(factor, 'col', axis=1, tiled=True)]
    mul x1 -> x0, other arithmetic: 4.86 us -> none  [masked(): block_rows.reshape(rblocks, bsz, width, bsz)]
    dot_general x1 -> x0, matrix products: 4.83 us -> none  [product(): jnp.dot(matrix, gather_rows(vector, cid), precision=lax.Precision.HIGHEST...]
  transfers between devices with their start and end apart: 1 -> 0, of which waited for: 1 -> 0; matrix products, arithmetic and copies ran while one was open for 3% -> 0% of each run, Pallas kernels for 17% -> 0%
where the time goes in v4:
time: 198 us
  Pallas kernels  181 us (91%)
  other arithmetic  7.95 us (4%)
  local copies, waits for them, and re-layouts  4.56 us (2%)
  matrix products  2.25 us (1%)
  between operations  2.07 us (1%)
    pallas_call x4, Pallas kernels, gather_product(): pl.pallas_call(functools.partial(gather_kernel, mode='fused'), out_shape=...  132 us
    pallas_call x1, Pallas kernels, first_product(): pl.pallas_call(functools.partial(gather_kernel, mode='first'), out_shape=...  49.5 us

profile of v4, /device:TPU:1, one launch (start us, length us, event | category | flops | bytes accessed | tf_op | source)
XLA Modules:
  0.0 197.9 jit_solution(2003707055715418987)
XLA Ops:
  0.0 0.0 copy-start.2
  0.0 0.8 select_reduce_fusion
  0.8 0.7 slice.3
  1.5 0.1 convert_reduce_fusion
  1.6 0.6 dynamic-slice
  2.2 0.6 fusion.15
  2.9 0.6 dynamic_slice.9
  5.4 0.7 compare_select_fusion
  6.1 1.3 gather_fusion
  7.4 0.9 fusion.2
  8.2 0.9 fusion.3
  9.1 0.3 fusion
  9.4 0.2 fusion.1
  9.6 0.7 broadcast_in_dim.77
  10.3 0.7 broadcast_in_dim.72
  11.0 49.5 %shard_map.64 = (f32[128,128]{1,0:T(8,128)}, f32[128,8192]{1,0:T(8,128)}) custom-call(f32[128,128]{1,0:T(8,128)} %refs_0_.1, f32[128,2048]{1,0:T(8,128)} %refs_1_.1, f32[1,8192]{1,0:T(1,128)} %bitcast.11), custom_call_target="tpu_custom_call" | custom-call | flops 268435456 | bytes 16777216 | tf_op jit(solution)/shard_map/pallas_call | solution.py:244
  60.5 1.5 broadcast_select_fusion.1.refs_0_
  61.9 32.4 %shard_map.65 = f32[128,128]{1,0:T(8,128)} custom-call(f32[128,128]{1,0:T(8,128)} %broadcast_select_fusion.1.refs_0_, f32[128,8192]{1,0:T(8,128)} %get-tuple-element.8.refs_1_, f32[1,8192]{1,0:T(1,128)} %bitcast.14), custom_call_target="tpu_custom_call" | custom-call | flops 268435456 | bytes 12582912 | tf_op jit(solution)/shard_map/pallas_call | solution.py:262
  94.3 0.0 copy-done.2
  94.3 1.5 sub.6.refs_0_
  95.8 0.0 copy-start
  95.8 32.7 %shard_map.66 = f32[128,128]{1,0:T(8,128)} custom-call(f32[128,128]{1,0:T(8,128)} %sub.6.refs_0_, f32[128,8192]{1,0:T(8,128)} %get-tuple-element.8.refs_1_, f32[1,8192]{1,0:T(1,128)} %bitcast.12), custom_call_target="tpu_custom_call" | custom-call | flops 268435456 | bytes 12582912 | tf_op jit(solution)/shard_map/pallas_call | solution.py:262
  128.5 0.6 broadcast_select_fusion.refs_0_
  129.2 0.0 copy-start.1
  129.2 0.0 copy-start.3
  129.2 34.2 %shard_map.67 = f32[128,128]{1,0:T(8,128)} custom-call(f32[128,128]{1,0:T(8,128)} %broadcast_select_fusion.refs_0_, f32[128,8192]{1,0:T(8,128)} %get-tuple-element.8.refs_1_, f32[1,8192]{1,0:T(1,128)} %bitcast.15), custom_call_target="tpu_custom_call" | custom-call | flops 268435456 | bytes 12582912 | tf_op jit(solution)/shard_map/pallas_call | solution.py:262
  163.4 0.0 copy-done
  163.4 1.5 add_subtract_fusion.refs_0_
  164.9 32.3 %shard_map.68 = f32[128,128]{1,0:T(8,128)} custom-call(f32[128,128]{1,0:T(8,128)} %add_subtract_fusion.refs_0_, f32[128,8192]{1,0:T(8,128)} %get-tuple-element.8.refs_1_, f32[1,8192]{1,0:T(1,128)} %bitcast.13), custom_call_target="tpu_custom_call" | custom-call | flops 268435456 | bytes 12582912 | tf_op jit(solution)/shard_map/pallas_call | solution.py:262
  197.2 0.0 copy-done.1
  197.3 0.0 copy-done.3
  197.3 0.7 select_add_fusion
  (3 shorter events, 0.0 us)
Async XLA Ops:
  0.0 94.3 %copy-start.2 = (f32[128,128]{1,0:T(8,128)S(1)}, f32[128,128]{1,0:T(8,128)}, u32[]{:S(2)}) copy-start(f32[128,128]{1,0:T(8,128)} %refs_0_.1) | copy-start | bytes 196612
  95.8 67.6 %copy-start = (f32[128,128]{1,0:T(8,128)S(1)}, f32[128,128]{1,0:T(8,128)}, u32[]{:S(2)}) copy-start(f32[128,128]{1,0:T(8,128)} %shard_map.65) | copy-start | bytes 196612
  129.2 68.1 %copy-start.1 = (f32[128,128]{1,0:T(8,128)S(1)}, f32[128,128]{1,0:T(8,128)}, u32[]{:S(2)}) copy-start(f32[128,128]{1,0:T(8,128)} %shard_map.66) | copy-start | bytes 196612
  129.2 68.1 %copy-start.3 = (f32[128,128]{1,0:T(8,128)S(1)}, f32[128,128]{1,0:T(8,128)}, u32[]{:S(2)}) copy-start(f32[128,128]{1,0:T(8,128)} %get-tuple-element.7) | copy-start | bytes 196612

commit v5 on v4

--- a/solution.py
+++ b/solution.py
@@ -13,40 +13,23 @@
 NY, NZ, NC = 4, 8, 2
 
 
-def block_masks(parent, bounds, slot, structure):
+def row_masks(parent, bounds, slot, structure, r):
     count = slot.shape[0]
     ar = jnp.arange(count, dtype=jnp.int32)
+    nodes = jnp.arange(parent.shape[0], dtype=jnp.int32)
     logical = jnp.sum(jnp.where(slot[:, None] == ar[None, :], ar[:, None], 0), axis=0)
     node = jnp.sum((logical[:, None] >= bounds[None, 1:7]).astype(jnp.int32), axis=1)
-    level = (node >= 4).astype(jnp.int32) + (node >= 6).astype(jnp.int32)
-    nodes = jnp.arange(7, dtype=jnp.int32)
-    grand = parent[parent]
-    ancestor = ((nodes[None, :] == parent[:, None]) | (nodes[None, :] == grand[:, None])) & (
-        nodes[None, :] != nodes[:, None]
-    )
-    node_hot = (node[:, None] == nodes[None, :]).astype(jnp.float32)
-    perm_hot = (logical[:, None] == ar[None, :]).astype(jnp.float32)
-    listed_store = jnp.dot(
-        structure.astype(jnp.float32), perm_hot.T, precision=lax.Precision.HIGHEST
-    )
-    anc_pairs = jnp.dot(
-        node_hot,
-        jnp.dot(ancestor.astype(jnp.float32), node_hot.T, precision=lax.Precision.HIGHEST),
-        precision=lax.Precision.HIGHEST,
-    )
-    list_pairs = jnp.dot(node_hot, listed_store, precision=lax.Precision.HIGHEST)
-    link = (anc_pairs * list_pairs).T > 0.5
-    same = node[:, None] == node[None, :]
-    return (level, same, link)
-
-
-def masked(block_rows, mask):
-    rblocks, width = mask.shape
-    bsz = block_rows.shape[0] // rblocks
-    shaped = block_rows.reshape(rblocks, bsz, width, bsz) * mask[:, None, :, None].astype(
-        jnp.float32
-    )
-    return shaped.reshape(block_rows.shape)
+    mine = ar == r
+    node_r = jnp.sum(jnp.where(mine, node, 0))
+    logical_r = jnp.sum(jnp.where(mine, logical, 0))
+    level_r = (node_r >= 4).astype(jnp.int32) + (node_r >= 6).astype(jnp.int32)
+    hot = node[:, None] == nodes[None, :]
+    par = jnp.sum(jnp.where(hot, parent[None, :], 0), axis=1)
+    grand = jnp.sum(jnp.where(par[:, None] == nodes[None, :], parent[None, :], 0), axis=1)
+    ancestor = ((par == node_r) | (grand == node_r)) & (node != node_r)
+    column = jnp.sum(jnp.where(ar[None, :] == logical_r, structure, 0), axis=1)
+    listed = jnp.sum(jnp.where(hot, column[None, :], 0), axis=1) == 1
+    return level_r, node == node_r, ancestor & listed
 
 
 def gather_kernel(*refs, mode):
@@ -275,19 +258,17 @@
 
 
 def body(factor, rhs, parent, bounds, slot, structure):
-    level, same, link = block_masks(parent, bounds, slot, structure)
-    first = lax.axis_index("row") * RB
-    level_mine = lax.dynamic_slice_in_dim(level, first, RB, 0)
-    same_row = jnp.repeat(lax.dynamic_slice_in_dim(same, first, RB, 0).astype(jnp.float32), B, axis=1)
-    link_row = jnp.repeat(lax.dynamic_slice_in_dim(link, first, RB, 0).astype(jnp.float32), B, axis=1)
-
-    rows0 = jnp.repeat(level_mine == 0, B)[:, None]
+    level_mine, same, link = row_masks(parent, bounds, slot, structure, lax.axis_index("row"))
+    same_row = jnp.repeat(same.astype(jnp.float32), B)[None, :]
+    link_row = jnp.repeat(link.astype(jnp.float32), B)[None, :]
+
+    rows0 = level_mine == 0
     first_prod, full_rows = first_product(factor, same_row, rhs, 0)
     solved = jnp.where(rows0, first_prod, 0.0)
     result = solved
     accum = gather_product(full_rows, link_row, solved, 1)
     for section in (1, 2):
-        rows = jnp.repeat(level_mine == section, B)[:, None]
+        rows = level_mine == section
         solved = jnp.where(rows, gather_product(full_rows, same_row, rhs - accum, 2 * section), 0.0)
         result = result + solved
         if section < 2:

time: 198 us -> 198 us (level)
  other arithmetic: 7.95 us -> 11 us
  local copies, waits for them, and re-layouts: 4.56 us -> 2.09 us
  matrix products: 2.25 us -> 0 us
  Pallas kernels: 181 us -> 183 us
    reduce_sum x2 -> x6, other arithmetic: 0.86 us -> 3.87 us  [the longest x1 0.8 us: row_masks(): column = jnp.sum(jnp.where(ar[None, :] == logical_r, structure, 0), axis=1)]
    dot_general x4 -> x0, matrix products: 2.25 us -> none  [the longest x1 0.88 us: block_masks(): jnp.dot(structure.astype(jnp.float32), perm_hot.T, precision=lax.Precisio...]
where the time goes in v5:
time: 198 us; the launch traced here: 197 us
  Pallas kernels  183 us (92%)
  other arithmetic  11 us (6%)
  local copies, waits for them, and re-layouts  2.09 us (1%)
    pallas_call x4, Pallas kernels, gather_product(): pl.pallas_call(functools.partial(gather_kernel, mode='fused'), out_shape=...  133 us
    pallas_call x1, Pallas kernels, first_product(): pl.pallas_call(functools.partial(gather_kernel, mode='first'), out_shape=...  49.5 us

profile of v5, /device:TPU:1, one launch (start us, length us, event | category | flops | bytes accessed | tf_op | source)
XLA Modules:
  0.0 197.2 jit_solution(3757840149329737536)
XLA Ops:
  0.0 0.0 copy-start.2
  0.0 0.8 select_reduce_fusion
  0.8 0.7 slice.3
  1.5 0.1 convert_reduce_fusion
  1.6 0.7 fusion
  3.6 0.7 iota_compare_fusion.3
  4.3 0.8 select_reduce_fusion.2
  5.1 0.7 select_reduce_fusion.4
  5.9 0.7 select_reduce_fusion.3
  6.6 0.6 and_convert_fusion
  7.3 0.7 broadcast_in_dim.86
  7.9 0.7 broadcast_in_dim.79
  8.6 49.5 %shard_map.64 = (f32[128,128]{1,0:T(8,128)}, f32[128,8192]{1,0:T(8,128)}) custom-call(f32[128,128]{1,0:T(8,128)} %refs_0_.1, f32[128,2048]{1,0:T(8,128)} %refs_1_.1, f32[1,8192]{1,0:T(1,128)} %bitcast.2), custom_call_target="tpu_custom_call" | custom-call | flops 268435456 | bytes 16777216 | tf_op jit(solution)/shard_map/pallas_call | solution.py:227
  58.1 1.5 broadcast_select_fusion.1.refs_0_
  59.6 32.7 %shard_map.65 = f32[128,128]{1,0:T(8,128)} custom-call(f32[128,128]{1,0:T(8,128)} %broadcast_select_fusion.1.refs_0_, f32[128,8192]{1,0:T(8,128)} %get-tuple-element.8.refs_1_, f32[1,8192]{1,0:T(1,128)} %bitcast.5), custom_call_target="tpu_custom_call" | custom-call | flops 268435456 | bytes 12582912 | tf_op jit(solution)/shard_map/pallas_call | solution.py:245
  92.3 0.0 copy-done.2
  92.3 1.5 sub.6.refs_0_
  93.7 0.0 copy-start
  93.7 33.5 %shard_map.66 = f32[128,128]{1,0:T(8,128)} custom-call(f32[128,128]{1,0:T(8,128)} %sub.6.refs_0_, f32[128,8192]{1,0:T(8,128)} %get-tuple-element.8.refs_1_, f32[1,8192]{1,0:T(1,128)} %bitcast.3), custom_call_target="tpu_custom_call" | custom-call | flops 268435456 | bytes 12582912 | tf_op jit(solution)/shard_map/pallas_call | solution.py:245
  127.3 0.6 broadcast_select_fusion.refs_0_
  127.9 0.0 copy-start.1
  127.9 0.0 copy-start.3
  127.9 32.8 %shard_map.67 = f32[128,128]{1,0:T(8,128)} custom-call(f32[128,128]{1,0:T(8,128)} %broadcast_select_fusion.refs_0_, f32[128,8192]{1,0:T(8,128)} %get-tuple-element.8.refs_1_, f32[1,8192]{1,0:T(1,128)} %bitcast.6), custom_call_target="tpu_custom_call" | custom-call | flops 268435456 | bytes 12582912 | tf_op jit(solution)/shard_map/pallas_call | solution.py:245
  160.7 0.0 copy-done
  160.7 1.5 add_subtract_fusion.refs_0_
  162.2 34.3 %shard_map.68 = f32[128,128]{1,0:T(8,128)} custom-call(f32[128,128]{1,0:T(8,128)} %add_subtract_fusion.refs_0_, f32[128,8192]{1,0:T(8,128)} %get-tuple-element.8.refs_1_, f32[1,8192]{1,0:T(1,128)} %bitcast.4), custom_call_target="tpu_custom_call" | custom-call | flops 268435456 | bytes 12582912 | tf_op jit(solution)/shard_map/pallas_call | solution.py:245
  196.5 0.0 copy-done.1
  196.5 0.0 copy-done.3
  196.5 0.7 select_add_fusion
Async XLA Ops:
  0.0 92.3 %copy-start.2 = (f32[128,128]{1,0:T(8,128)S(1)}, f32[128,128]{1,0:T(8,128)}, u32[]{:S(2)}) copy-start(f32[128,128]{1,0:T(8,128)} %refs_0_.1) | copy-start | bytes 196612
  93.7 67.0 %copy-start = (f32[128,128]{1,0:T(8,128)S(1)}, f32[128,128]{1,0:T(8,128)}, u32[]{:S(2)}) copy-start(f32[128,128]{1,0:T(8,128)} %shard_map.65) | copy-start | bytes 196612
  127.9 68.6 %copy-start.1 = (f32[128,128]{1,0:T(8,128)S(1)}, f32[128,128]{1,0:T(8,128)}, u32[]{:S(2)}) copy-start(f32[128,128]{1,0:T(8,128)} %shard_map.66) | copy-start | bytes 196612
  127.9 68.6 %copy-start.3 = (f32[128,128]{1,0:T(8,128)S(1)}, f32[128,128]{1,0:T(8,128)}, u32[]{:S(2)}) copy-start(f32[128,128]{1,0:T(8,128)} %get-tuple-element.7) | copy-start | bytes 196612

commit v6 on v5

--- a/solution.py
+++ b/solution.py
@@ -206,6 +206,128 @@
     out_ref[...] = acc[...]
 
 
+def split_kernel(x_ref, fo_ref, fp_ref, mo_ref, mp_ref, oo_ref, op_ref, G, acc_o, acc_p, local_sem, send_sem,
+                 recv_z, recv_y):
+    nb, w = x_ref.shape
+    r = lax.axis_index("row")
+    c = lax.axis_index("col")
+    y = r // (NZ * NC)
+    z = (r // NC) % NZ
+    k = r % NC
+
+    def dev(yy, zz):
+        return (((yy + NY) % NY) * NZ + (zz + NZ) % NZ) * NC + k
+
+    def blk(yy, zz):
+        return G.at[((yy + NY) % NY) * NZ + (zz + NZ) % NZ]
+
+    zr, zl, yr, yl = dev(y, z + 1), dev(y, z - 1), dev(y + 1, z), dev(y - 1, z)
+    barrier = pltpu.get_barrier_semaphore()
+    for d in (zr, zl, yr, yl):
+        pl.semaphore_signal(barrier, inc=1, device_id=(d, c), device_id_type=MESH)
+    pl.semaphore_wait(barrier, 4)
+
+    local = pltpu.make_async_copy(x_ref, blk(y, z), local_sem.at[0])
+    local.start()
+    sends = []
+
+    def remote(src, dst, rsem, d, si=0):
+        return pltpu.make_async_remote_copy(
+            src_ref=src, dst_ref=dst, send_sem=send_sem.at[si], recv_sem=rsem,
+            device_id=(d, c), device_id_type=MESH,
+        )
+
+    def send(src, dst, rsem, d):
+        cp = remote(src, dst, rsem, d, len(sends))
+        cp.start()
+        sends.append(cp)
+
+    def wait(ref, rsem):
+        remote(ref, ref, rsem, zr).wait_recv()
+
+    def recv_of(zsrc):
+        return recv_z.at[(zsrc + NZ) % NZ]
+
+    offs = [0, -1, 1, -2, 2, -3, 3, -4]
+    to_right = {0, -1, -2, -3}
+
+    def spread(off):
+        i = offs.index(off)
+        ref = x_ref if off == 0 else blk(y, z + off)
+        send(ref, blk(y, z + off), recv_y.at[0, i], yr)
+        send(ref, blk(y, z + off), recv_y.at[1, i], yl)
+
+    for s in range(4):
+        if s >= 1:
+            wait(blk(y, z - s), recv_of(z - s))
+        send(x_ref if s == 0 else blk(y, z - s), blk(y, z - s), recv_of(z - s), zr)
+        if s < 3:
+            if s >= 1:
+                wait(blk(y, z + s), recv_of(z + s))
+            send(x_ref if s == 0 else blk(y, z + s), blk(y, z + s), recv_of(z + s), zl)
+        if s == 0:
+            spread(0)
+        else:
+            spread(-s)
+            if s < 3:
+                spread(s)
+    wait(blk(y, z - 4), recv_of(z - 4))
+    spread(-4)
+    wait(blk(y, z + 3), recv_of(z + 3))
+    spread(3)
+    for i, off in enumerate(offs):
+        wait(blk(y - 1, z + off), recv_y.at[0, i])
+        if off in to_right:
+            send(blk(y - 1, z + off), blk(y - 1, z + off), recv_y.at[2, i], yr)
+        wait(blk(y + 1, z + off), recv_y.at[1, i])
+        if off not in to_right:
+            send(blk(y + 1, z + off), blk(y + 1, z + off), recv_y.at[3, i], yl)
+    local.wait()
+    acc_o[...] = jnp.zeros_like(acc_o)
+    acc_p[...] = jnp.zeros_like(acc_p)
+
+    def multiply(yy):
+        plane = (yy + NY) % NY
+        cols = pl.ds(pl.multiple_of(plane * (NZ * nb), nb), NZ * nb)
+        vec = G[pl.ds(plane * NZ, NZ)].reshape(NZ * nb, w)
+        acc_o[...] += jnp.dot(fo_ref[:, cols] * mo_ref[:, cols], vec,
+                              precision=lax.Precision.HIGHEST, preferred_element_type=jnp.float32)
+        acc_p[...] += jnp.dot(fp_ref[:, cols] * mp_ref[:, cols], vec,
+                              precision=lax.Precision.HIGHEST, preferred_element_type=jnp.float32)
+
+    multiply(y)
+    multiply(y - 1)
+    multiply(y + 1)
+    for i, off in enumerate(offs):
+        wait(blk(y + 2, z + off), recv_y.at[2 if off in to_right else 3, i])
+    multiply(y + 2)
+    for cp in sends:
+        cp.wait_send()
+    oo_ref[...] = acc_o[...]
+    op_ref[...] = acc_p[...]
+
+
+def split_product(fo, fp, mo, mp, x, cid):
+    nb, w = x.shape
+    rows = fo.shape[0]
+    out = jax.ShapeDtypeStruct((rows, w), jnp.float32)
+    return pl.pallas_call(
+        split_kernel,
+        out_shape=(out, out),
+        in_specs=_specs(5),
+        out_specs=(pl.BlockSpec(memory_space=pltpu.VMEM), pl.BlockSpec(memory_space=pltpu.VMEM)),
+        scratch_shapes=[pltpu.VMEM((NY * NZ, nb, w), x.dtype), pltpu.VMEM((rows, w), jnp.float32),
+                        pltpu.VMEM((rows, w), jnp.float32), pltpu.SemaphoreType.DMA((1,)),
+                        pltpu.SemaphoreType.DMA((40,)), pltpu.SemaphoreType.DMA((NZ,)),
+                        pltpu.SemaphoreType.DMA((4, NZ))],
+        compiler_params=pltpu.CompilerParams(collective_id=cid, has_side_effects=True),
+        cost_estimate=pl.CostEstimate(
+            flops=4 * rows * fo.shape[1] * w, transcendentals=0,
+            bytes_accessed=(2 * fo.size + x.size * 64) * 4,
+        ),
+    )(x, fo, fp, mo, mp)
+
+
 def _sems():
     return [
         pltpu.SemaphoreType.DMA((2,)),
@@ -258,7 +380,9 @@
 
 
 def body(factor, rhs, parent, bounds, slot, structure):
-    level_mine, same, link = row_masks(parent, bounds, slot, structure, lax.axis_index("row"))
+    r = lax.axis_index("row")
+    level_mine, same, link = row_masks(parent, bounds, slot, structure, r)
+    _, same_p, link_p = row_masks(parent, bounds, slot, structure, r + 1 - 2 * (r % NC))
     same_row = jnp.repeat(same.astype(jnp.float32), B)[None, :]
     link_row = jnp.repeat(link.astype(jnp.float32), B)[None, :]
 
@@ -266,13 +390,34 @@
     first_prod, full_rows = first_product(factor, same_row, rhs, 0)
     solved = jnp.where(rows0, first_prod, 0.0)
     result = solved
-    accum = gather_product(full_rows, link_row, solved, 1)
+
+    k = r % NC
+    pairs = [(i, i + 1 - 2 * (i % NC)) for i in range(NY * NZ * NC)]
+
+    def classes(a):
+        return a.reshape(a.shape[0], NY * NZ, NC, B)
+
+    def pick(a, kk):
+        return lax.dynamic_index_in_dim(classes(a), kk, axis=2, keepdims=False).reshape(a.shape[0], -1)
+
+    f_own = pick(full_rows, k)
+    f_part = lax.ppermute(pick(full_rows, 1 - k), "row", pairs)
+    masks = {
+        "same": (pick(same_row, k), pick(jnp.repeat(same_p.astype(jnp.float32), B)[None, :], k)),
+        "link": (pick(link_row, k), pick(jnp.repeat(link_p.astype(jnp.float32), B)[None, :], k)),
+    }
+
+    def product(kind, x, cid):
+        own, part = split_product(f_own, f_part, masks[kind][0], masks[kind][1], x, cid)
+        return own + lax.ppermute(part, "row", pairs)
+
+    accum = product("link", solved, 1)
     for section in (1, 2):
         rows = level_mine == section
-        solved = jnp.where(rows, gather_product(full_rows, same_row, rhs - accum, 2 * section), 0.0)
+        solved = jnp.where(rows, product("same", rhs - accum, 2 * section), 0.0)
         result = result + solved
         if section < 2:
-            accum = accum + gather_product(full_rows, link_row, solved, 2 * section + 1)
+            accum = accum + product("link", solved, 2 * section + 1)
     return result
 
 

time: 198 us -> 219 us (1.11)
  Pallas kernels: 183 us -> 157 us
  local copies, waits for them, and re-layouts: 2.09 us -> 25.7 us
  starting transfers between devices: 0 us -> 18.4 us
  waiting for transfers between devices: 0 us -> 3.88 us
    pallas_call x4, Pallas kernels: 133 us -> 107 us  [split_product(): pl.pallas_call(split_kernel, out_shape=(out, out), in_specs=_specs(5), ou...]
    ppermute x0 -> x5, starting transfers between devices: none -> 18.4 us  [the longest x4 16.2 us: product(): return own + lax.ppermute(part, 'row', pairs)]
    dynamic_slice x0 -> x5, local copies, waits for them, and re-layouts: none -> 8.63 us  [pick(): lax.dynamic_index_in_dim(classes(a), kk, axis=2, keepdims=False)]
    reshape x0 -> x1, local copies, waits for them, and re-layouts: none -> 6.58 us  [classes(): return a.reshape(a.shape[0], NY * NZ, NC, B)]
    unnamed x8 -> x10, local copies, waits for them, and re-layouts: 0.01 us -> 5.93 us
    ppermute x0 -> x5, waiting for transfers between devices: none -> 3.88 us  [the longest x4 3.87 us: product(): return own + lax.ppermute(part, 'row', pairs)]
  transfers between devices with their start and end apart: 0 -> 5, of which waited for: 0 -> 4; matrix products, arithmetic and copies ran while one was open for 0% -> 2% of each run, Pallas kernels for 0% -> 0%
where the time goes in v6:
time: 219 us
  Pallas kernels  157 us (72%)
  local copies, waits for them, and re-layouts  25.7 us (12%)
  starting transfers between devices  18.4 us (8%)
  other arithmetic  12.9 us (6%)
  waiting for transfers between devices  3.88 us (2%)
    pallas_call x4, Pallas kernels, split_product(): pl.pallas_call(split_kernel, out_shape=(out, out), in_specs=_specs(5), ou...  107 us
    pallas_call x1, Pallas kernels, first_product(): pl.pallas_call(functools.partial(gather_kernel, mode='first'), out_shape=...  49.5 us
    ppermute x4, starting transfers between devices, product(): return own + lax.ppermute(part, 'row', pairs)  16.2 us
    dynamic_slice x5, local copies, waits for them, and re-layouts, pick(): lax.dynamic_index_in_dim(classes(a), kk, axis=2, keepdims=False)  8.63 us
    reshape x1, local copies, waits for them, and re-layouts, classes(): return a.reshape(a.shape[0], NY * NZ, NC, B)  6.58 us
    unnamed x10, local copies, waits for them, and re-layouts  5.93 us
  transfers between devices with their start and end apart: 5, of which 4 were waited for; matrix products, arithmetic and copies ran while one was open for 2% of the time, Pallas kernels for 0%

profile of v6, /device:TPU:1, one launch (start us, length us, event | category | flops | bytes accessed | tf_op | source)
XLA Modules:
  0.0 218.7 jit_solution(1664282657765102931)
XLA Ops:
  0.0 0.7 select_reduce_fusion
  0.7 0.7 slice.4
  1.5 0.1 convert_reduce_fusion
  1.6 0.7 fusion.2
  2.3 0.6 iota_compare_fusion.3
  2.9 0.7 iota_compare_fusion.4
  3.6 0.8 select_reduce_fusion.2
  4.4 0.8 select_reduce_fusion.1
  5.2 0.7 select_reduce_fusion.5
  5.9 1.2 and_convert_fusion
  7.1 0.7 broadcast_in_dim.134
  7.8 49.5 %shard_map.64 = (f32[128,128]{1,0:T(8,128)}, f32[128,8192]{1,0:T(8,128)}) custom-call(f32[128,128]{1,0:T(8,128)} %refs_0_.1, f32[128,2048]{1,0:T(8,128)} %refs_1_.1, f32[1,8192]{1,0:T(1,128)} %bitcast.33), custom_call_target="tpu_custom_call" | custom-call | flops 268435456 | bytes 16777216 | tf_op jit(solution)/shard_map/pallas_call | solution.py:349
  57.3 6.6 %reshape.110 = f32[128,32,2,128]{3,2,1,0:T(2,128)} reshape(f32[128,8192]{1,0:T(8,128)} %get-tuple-element.16) | data formatting | bytes 8388608 | tf_op jit(solution)/shard_map/reshape | solution.py:398
  63.8 7.9 %constant_dynamic-slice_fusion = (f32[128,32,1,128]{3,2,1,0:T(1,128)S(1)}, f32[128,32,1,128]{3,2,1,0:T(1,128)S(1)}) fusion(f32[128,32,2,128]{3,2,1,0:T(2,128)} %reshape.110, s32[]{:T(128)S(6)} %select_n.88, s32[]{:T(128)S(6)} %select_n.87), kind=kLoop, calls=%fused_computation.25 | loop fusion | bytes 8388616 | tf_op jit(solution)/shard_map/jit(dynamic_index_in_dim)/dynamic_slice | solution.py:401
  71.7 2.9 %copy.19 = f32[16,8,32,128]{3,1,2,0:T(8,128)} copy(f32[16,8,32,128]{3,2,1,0:T(8,128)S(1)} %bitcast.24) | data formatting | bytes 4194304
  74.7 2.2 %collective-permute-start = (f32[128,4096]{1,0:T(8,128)}, f32[128,4096]{1,0:T(8,128)S(1)}, u32[]{:S(2)}, u32[]{:S(2)}) collective-permute-start(f32[128,4096]{1,0:T(8,128)} %bitcast.17), channel_id=1, source_target_pairs={{0,4},{4,0},{8,12},{12,8},{16,20},{20,16},{24,28},{28,24},{32,36},... | collective-permute-start | bytes 6291464 | tf_op jit(solution)/shard_map/ppermute | solution.py:404
  76.9 3.0 %copy.20 = f32[16,8,32,128]{3,1,2,0:T(8,128)} copy(f32[16,8,32,128]{3,2,1,0:T(8,128)S(1)} %bitcast.23) | data formatting | bytes 4194304
  81.0 0.1 reshape.113
  81.1 0.1 reshape.114
  81.2 0.2 dynamic-slice_reduce_fusion.3
  81.4 0.2 dynamic-slice_reduce_fusion.2
  81.5 0.0 copy-done.3
  81.5 0.6 broadcast_select_fusion.x_ref
  82.2 0.0 collective-permute-done.fp_ref
  82.2 0.8 broadcast_in_dim.141
  83.0 0.7 broadcast_in_dim.145
  83.6 26.8 %shard_map.65 = (f32[128,128]{1,0:T(8,128)}, f32[128,128]{1,0:T(8,128)}) custom-call(f32[128,128]{1,0:T(8,128)} %broadcast_select_fusion.x_ref, f32[128,4096]{1,0:T(8,128)} %bitcast.19, f32[128,4096]{1,0:T(8,128)} %copy-done, f32[1,4096]{1,0:T(1,128)} %bitcast.25, f32[1,4096]{1,0:T(1,128)} %bitcast.27), custom_call_target="tpu_custom_call" | custom-call | flops 268435456 | bytes 8388608 | tf_op jit(solution)/shard_map/pallas_call | solution.py:314
  110.4 3.7 %collective-permute-start.1 = (f32[128,128]{1,0:T(8,128)}, f32[128,128]{1,0:T(8,128)S(1)}, u32[]{:S(2)}, u32[]{:S(2)}) collective-permute-start(f32[128,128]{1,0:T(8,128)} %get-tuple-element.18), channel_id=1, source_target_pairs={{0,4},{4,0},{8,12},{12,8},{16,20},{20,16},{24,28},{28,24},{32,36},... | collective-permute-start | bytes 196616 | tf_op jit(solution)/shard_map/ppermute | solution.py:412
  114.1 0.1 reshape.115
  114.2 0.1 reshape.116
  114.3 0.2 dynamic-slice_reduce_fusion.1
  114.5 0.2 dynamic-slice_reduce_fusion
  114.7 0.5 collective-permute-done.1
  115.2 1.5 fusion.4
  116.7 0.7 broadcast_in_dim.147
  117.4 0.7 broadcast_in_dim.149
  118.1 27.0 %shard_map.66 = (f32[128,128]{1,0:T(8,128)}, f32[128,128]{1,0:T(8,128)}) custom-call(f32[128,128]{1,0:T(8,128)} %get-tuple-element.34.x_ref, f32[128,4096]{1,0:T(8,128)} %bitcast.20, f32[128,4096]{1,0:T(8,128)} %copy-done, f32[1,4096]{1,0:T(1,128)} %bitcast.29, f32[1,4096]{1,0:T(1,128)} %bitcast.31), custom_call_target="tpu_custom_call" | custom-call | flops 268435456 | bytes 8388608 | tf_op jit(solution)/shard_map/pallas_call | solution.py:314
  145.1 4.2 %collective-permute-start.2 = (f32[128,128]{1,0:T(8,128)}, f32[128,128]{1,0:T(8,128)S(1)}, u32[]{:S(2)}, u32[]{:S(2)}) collective-permute-start(f32[128,128]{1,0:T(8,128)} %get-tuple-element.20), channel_id=1, source_target_pairs={{0,4},{4,0},{8,12},{12,8},{16,20},{20,16},{24,28},{28,24},{32,36},... | collective-permute-start | bytes 196616 | tf_op jit(solution)/shard_map/ppermute | solution.py:412
  149.3 1.1 collective-permute-done.2
  150.4 1.5 add_select_fusion.x_ref
  151.9 26.9 %shard_map.67 = (f32[128,128]{1,0:T(8,128)}, f32[128,128]{1,0:T(8,128)}) custom-call(f32[128,128]{1,0:T(8,128)} %add_select_fusion.x_ref, f32[128,4096]{1,0:T(8,128)} %bitcast.21, f32[128,4096]{1,0:T(8,128)} %copy-done, f32[1,4096]{1,0:T(1,128)} %bitcast.26, f32[1,4096]{1,0:T(1,128)} %bitcast.28), custom_call_target="tpu_custom_call" | custom-call | flops 268435456 | bytes 8388608 | tf_op jit(solution)/shard_map/pallas_call | solution.py:314
  178.8 4.2 %collective-permute-start.3 = (f32[128,128]{1,0:T(8,128)}, f32[128,128]{1,0:T(8,128)S(1)}, u32[]{:S(2)}, u32[]{:S(2)}) collective-permute-start(f32[128,128]{1,0:T(8,128)} %get-tuple-element.22), channel_id=1, source_target_pairs={{0,4},{4,0},{8,12},{12,8},{16,20},{20,16},{24,28},{28,24},{32,36},... | collective-permute-start | bytes 196616 | tf_op jit(solution)/shard_map/ppermute | solution.py:412
  182.9 1.1 collective-permute-done.3
  184.1 1.5 add_subtract_fusion.x_ref
  185.5 26.5 %shard_map.68 = (f32[128,128]{1,0:T(8,128)}, f32[128,128]{1,0:T(8,128)}) custom-call(f32[128,128]{1,0:T(8,128)} %add_subtract_fusion.x_ref, f32[128,4096]{1,0:T(8,128)} %bitcast.22, f32[128,4096]{1,0:T(8,128)} %copy-done, f32[1,4096]{1,0:T(1,128)} %bitcast.30, f32[1,4096]{1,0:T(1,128)} %bitcast.32), custom_call_target="tpu_custom_call" | custom-call | flops 268435456 | bytes 8388608 | tf_op jit(solution)/shard_map/pallas_call | solution.py:314
  212.0 4.1 %collective-permute-start.4 = (f32[128,128]{1,0:T(8,128)}, f32[128,128]{1,0:T(8,128)S(1)}, u32[]{:S(2)}, u32[]{:S(2)}) collective-permute-start(f32[128,128]{1,0:T(8,128)} %get-tuple-element.24), channel_id=1, source_target_pairs={{0,4},{4,0},{8,12},{12,8},{16,20},{20,16},{24,28},{28,24},{32,36},... | collective-permute-start | bytes 196616 | tf_op jit(solution)/shard_map/ppermute | solution.py:412
  216.1 1.1 collective-permute-done.4
  217.3 1.5 select_add_fusion
  (7 shorter events, 0.0 us)
Async XLA Ops:
  74.7 7.5 %collective-permute-start = (f32[128,4096]{1,0:T(8,128)}, f32[128,4096]{1,0:T(8,128)S(1)}, u32[]{:S(2)}, u32[]{:S(2)}) collective-permute-start(f32[128,4096]{1,0:T(8,128)} %bitcast.17), channel_id=1, source_target_pairs={{0,4},{4,0},{8,12},{12,8},{16,20},{20,16},{24,28},{28,24},{32,36},... | collective-permute-start | bytes 6291464 | tf_op jit(solution)/shard_map/ppermute | solution.py:404
  76.9 4.7 %copy-start.3 = (f32[128,128]{1,0:T(8,128)S(1)}, f32[128,128]{1,0:T(8,128)}, u32[]{:S(2)}) copy-start(f32[128,128]{1,0:T(8,128)} %get-tuple-element.15) | copy-start | bytes 196612
  82.2 1.4 copy-start
  83.6 31.6 %copy-start.2 = (f32[128,128]{1,0:T(8,128)S(1)}, f32[128,128]{1,0:T(8,128)}, u32[]{:S(2)}) copy-start(f32[128,128]{1,0:T(8,128)} %refs_0_.1) | copy-start | bytes 196612
  110.4 4.8 %collective-permute-start.1 = (f32[128,128]{1,0:T(8,128)}, f32[128,128]{1,0:T(8,128)S(1)}, u32[]{:S(2)}, u32[]{:S(2)}) collective-permute-start(f32[128,128]{1,0:T(8,128)} %get-tuple-element.18), channel_id=1, source_target_pairs={{0,4},{4,0},{8,12},{12,8},{16,20},{20,16},{24,28},{28,24},{32,36},... | collective-permute-start | bytes 196616 | tf_op jit(solution)/shard_map/ppermute | solution.py:412
  145.1 5.3 %collective-permute-start.2 = (f32[128,128]{1,0:T(8,128)}, f32[128,128]{1,0:T(8,128)S(1)}, u32[]{:S(2)}, u32[]{:S(2)}) collective-permute-start(f32[128,128]{1,0:T(8,128)} %get-tuple-element.20), channel_id=1, source_target_pairs={{0,4},{4,0},{8,12},{12,8},{16,20},{20,16},{24,28},{28,24},{32,36},... | collective-permute-start | bytes 196616 | tf_op jit(solution)/shard_map/ppermute | solution.py:412
  178.8 5.3 %collective-permute-start.3 = (f32[128,128]{1,0:T(8,128)}, f32[128,128]{1,0:T(8,128)S(1)}, u32[]{:S(2)}, u32[]{:S(2)}) collective-permute-start(f32[128,128]{1,0:T(8,128)} %get-tuple-element.22), channel_id=1, source_target_pairs={{0,4},{4,0},{8,12},{12,8},{16,20},{20,16},{24,28},{28,24},{32,36},... | collective-permute-start | bytes 196616 | tf_op jit(solution)/shard_map/ppermute | solution.py:412
  185.5 31.7 %copy-start.1 = (f32[128,128]{1,0:T(8,128)S(1)}, f32[128,128]{1,0:T(8,128)}, u32[]{:S(2)}) copy-start(f32[128,128]{1,0:T(8,128)} %add_select_fusion.x_ref) | copy-start | bytes 196612
  212.0 5.2 %collective-permute-start.4 = (f32[128,128]{1,0:T(8,128)}, f32[128,128]{1,0:T(8,128)S(1)}, u32[]{:S(2)}, u32[]{:S(2)}) collective-permute-start(f32[128,128]{1,0:T(8,128)} %get-tuple-element.24), channel_id=1, source_target_pairs={{0,4},{4,0},{8,12},{12,8},{16,20},{20,16},{24,28},{28,24},{32,36},... | collective-permute-start | bytes 196616 | tf_op jit(solution)/shard_map/ppermute | solution.py:412

commit v7 on v5

--- a/solution.py
+++ b/solution.py
@@ -32,13 +32,16 @@
     return level_r, node == node_r, ancestor & listed
 
 
-def gather_kernel(*refs, mode):
+def gather_kernel(*refs, mode, epilogue=None, n_extra=0, n_out=1):
     fused = True
     if mode == "first":
         x_ref, floc_ref, m_ref, out_ref, fout_ref, G, f_ref, acc, local_sem, send_sem, recv_z, recv_y, recv_c, \
             recv_x = refs
     else:
-        x_ref, f_ref, m_ref, out_ref, G, acc, local_sem, send_sem, recv_z, recv_y, recv_c = refs
+        x_ref, f_ref, m_ref = refs[:3]
+        extra_refs = refs[3:3 + n_extra]
+        out_refs = refs[3 + n_extra:3 + n_extra + n_out]
+        G, acc, local_sem, send_sem, recv_z, recv_y, recv_c = refs[3 + n_extra + n_out:]
     nb, w = x_ref.shape
     r = lax.axis_index("row")
     c = lax.axis_index("col")
@@ -203,7 +206,11 @@
 
     for cp in sends:
         cp.wait_send()
-    out_ref[...] = acc[...]
+    if mode == "first":
+        out_ref[...] = acc[...]
+    else:
+        for ref, value in zip(out_refs, epilogue(acc[...], *[e[...] for e in extra_refs])):
+            ref[...] = value
 
 
 def _sems():
@@ -239,14 +246,15 @@
     )(x, floc, mask_row)
 
 
-def gather_product(matrix, mask_row, x, cid):
+def gather_product(matrix, mask_row, x, cid, extras, epilogue, n_out):
     nb, w = x.shape
     shape = (NY * NZ, NC, nb, w)
+    out = jax.ShapeDtypeStruct((matrix.shape[0], w), jnp.float32)
     return pl.pallas_call(
-        functools.partial(gather_kernel, mode="fused"),
-        out_shape=jax.ShapeDtypeStruct((matrix.shape[0], w), jnp.float32),
-        in_specs=_specs(3),
-        out_specs=pl.BlockSpec(memory_space=pltpu.VMEM),
+        functools.partial(gather_kernel, mode="fused", epilogue=epilogue, n_extra=len(extras), n_out=n_out),
+        out_shape=tuple([out] * n_out),
+        in_specs=_specs(3 + len(extras)),
+        out_specs=tuple(pl.BlockSpec(memory_space=pltpu.VMEM) for _ in range(n_out)),
         scratch_shapes=[pltpu.VMEM(shape, x.dtype), pltpu.VMEM((matrix.shape[0], w), jnp.float32)]
         + _sems(),
         compiler_params=pltpu.CompilerParams(collective_id=cid, has_side_effects=True),
@@ -254,7 +262,17 @@
             flops=2 * matrix.shape[0] * matrix.shape[1] * w, transcendentals=0,
             bytes_accessed=(matrix.size + 2 * x.size * 64) * 4,
         ),
-    )(x, matrix, mask_row)
+    )(x, matrix, mask_row, *extras)
+
+
+def _link_epilogue(prod, accum, rhs):
+    accum = accum + prod
+    return accum, rhs - accum
+
+
+def _diag_epilogue(prod, sel, result):
+    solved = jnp.where(sel > 0.5, prod, 0.0)
+    return solved, result + solved
 
 
 def body(factor, rhs, parent, bounds, slot, structure):
@@ -266,13 +284,14 @@
     first_prod, full_rows = first_product(factor, same_row, rhs, 0)
     solved = jnp.where(rows0, first_prod, 0.0)
     result = solved
-    accum = gather_product(full_rows, link_row, solved, 1)
+    accum = jnp.zeros(rhs.shape, jnp.float32)
+    accum, vector = gather_product(full_rows, link_row, solved, 1, (accum, rhs), _link_epilogue, 2)
     for section in (1, 2):
-        rows = level_mine == section
-        solved = jnp.where(rows, gather_product(full_rows, same_row, rhs - accum, 2 * section), 0.0)
-        result = result + solved
+        sel = jnp.full((1, rhs.shape[1]), (level_mine == section).astype(jnp.float32))
+        solved, result = gather_product(full_rows, same_row, vector, 2 * section, (sel, result), _diag_epilogue, 2)
         if section < 2:
-            accum = accum + gather_product(full_rows, link_row, solved, 2 * section + 1)
+            accum, vector = gather_product(full_rows, link_row, solved, 2 * section + 1, (accum, rhs),
+                                           _link_epilogue, 2)
     return result
 
 

time: 198 us -> 193 us (0.975)
  other arithmetic: 11 us -> 6.66 us
  local copies, waits for them, and re-layouts: 2.09 us -> 5.22 us
  Pallas kernels: 183 us -> 180 us
    sub x2 -> x0, other arithmetic: 2.96 us -> none  [body(): rhs - accum]
    pallas_call x4, Pallas kernels: 133 us -> 130 us  [gather_product(): pl.pallas_call(functools.partial(gather_kernel, mode='fused', epilogue=ep...]
where the time goes in v7:
time: 193 us
  Pallas kernels  180 us (93%)
  other arithmetic  6.66 us (3%)
  local copies, waits for them, and re-layouts  5.22 us (3%)
    pallas_call x4, Pallas kernels, gather_product(): pl.pallas_call(functools.partial(gather_kernel, mode='fused', epilogue=ep...  130 us
    pallas_call x1, Pallas kernels, first_product(): pl.pallas_call(functools.partial(gather_kernel, mode='first'), out_shape=...  49.5 us

profile of v7, /device:TPU:1, one launch (start us, length us, event | category | flops | bytes accessed | tf_op | source)
XLA Modules:
  0.0 193.1 jit_solution(9431956440909530700)
XLA Ops:
  0.0 0.7 select_reduce_fusion
  0.7 0.7 slice.3
  1.5 0.1 convert_reduce_fusion
  1.6 0.7 fusion
  3.6 0.5 broadcast_in_dim.92.refs_3_
  4.1 0.5 broadcast_in_dim.93.refs_3_
  4.6 0.7 iota_compare_fusion.3
  5.3 0.8 select_reduce_fusion.2
  6.1 0.7 select_reduce_fusion.4
  6.9 0.7 select_reduce_fusion.3
  7.6 0.6 and_convert_fusion
  8.3 0.7 broadcast_in_dim.91
  8.9 0.7 broadcast_in_dim.84
  9.6 49.5 %shard_map.64 = (f32[128,128]{1,0:T(8,128)}, f32[128,8192]{1,0:T(8,128)}) custom-call(f32[128,128]{1,0:T(8,128)} %refs_4_.3, f32[128,2048]{1,0:T(8,128)} %refs_1_.1, f32[1,8192]{1,0:T(1,128)} %bitcast.2), custom_call_target="tpu_custom_call" | custom-call | flops 268435456 | bytes 16777216 | tf_op jit(solution)/shard_map/pallas_call | solution.py:234
  59.1 1.5 broadcast_select_fusion.refs_0_.refs_4_
  60.6 0.6 broadcast_in_dim.85.refs_3_
  61.2 33.0 %shard_map.65 = (f32[128,128]{1,0:T(8,128)}, f32[128,128]{1,0:T(8,128)}) custom-call(f32[128,128]{1,0:T(8,128)} %broadcast_select_fusion.refs_0_.refs_4_, f32[128,8192]{1,0:T(8,128)} %get-tuple-element.14.refs_1_, f32[1,8192]{1,0:T(1,128)} %bitcast.5, f32[128,128]{1,0:T(8,128)} %broadcast_in_dim.85.refs_3_, f32[128,128]{1,0:T(8,128)} %refs_4_.3), custom_call_target="tpu_custom_call" | custom-call | flops 268435456 | bytes 12582912 | tf_op jit(solution)/shard_map/pallas_call | solution.py:253
  94.2 32.9 %shard_map.66 = (f32[128,128]{1,0:T(8,128)}, f32[128,128]{1,0:T(8,128)}) custom-call(f32[128,128]{1,0:T(8,128)} %get-tuple-element.15.refs_0_, f32[128,8192]{1,0:T(8,128)} %get-tuple-element.14.refs_1_, f32[1,8192]{1,0:T(1,128)} %bitcast.3, f32[1,128]{1,0:T(1,128)} %broadcast_in_dim.92.refs_3_, f32[128,128]{1,0:T(8,128)} %broadcast_select_fusion.refs_0_.refs_4_), custom_call_target="tpu_custom_call" | custom-call | flops 268435456 | bytes 12582912 | tf_op jit(solution)/shard_map/pallas_call | solution.py:253
  127.1 32.0 %shard_map.67 = (f32[128,128]{1,0:T(8,128)}, f32[128,128]{1,0:T(8,128)}) custom-call(f32[128,128]{1,0:T(8,128)} %get-tuple-element.16.refs_0_, f32[128,8192]{1,0:T(8,128)} %get-tuple-element.14.refs_1_, f32[1,8192]{1,0:T(1,128)} %bitcast.6, f32[128,128]{1,0:T(8,128)} %get-tuple-element.17.refs_3_, f32[128,128]{1,0:T(8,128)} %refs_4_.3), custom_call_target="tpu_custom_call" | custom-call | flops 268435456 | bytes 12582912 | tf_op jit(solution)/shard_map/pallas_call | solution.py:253
  159.2 32.5 %shard_map.68 = (f32[128,128]{1,0:T(8,128)}, f32[128,128]{1,0:T(8,128)}) custom-call(f32[128,128]{1,0:T(8,128)} %get-tuple-element.18.refs_0_, f32[128,8192]{1,0:T(8,128)} %get-tuple-element.14.refs_1_, f32[1,8192]{1,0:T(1,128)} %bitcast.4, f32[1,128]{1,0:T(1,128)} %broadcast_in_dim.93.refs_3_, f32[128,128]{1,0:T(8,128)} %get-tuple-element.19.refs_4_), custom_call_target="tpu_custom_call" | custom-call | flops 268435456 | bytes 12582912 | tf_op jit(solution)/shard_map/pallas_call | solution.py:253
  191.7 1.5 copy.8

commit v8 on v7

--- a/solution.py
+++ b/solution.py
@@ -35,7 +35,7 @@
 def gather_kernel(*refs, mode, epilogue=None, n_extra=0, n_out=1):
     fused = True
     if mode == "first":
-        x_ref, floc_ref, m_ref, out_ref, fout_ref, G, f_ref, acc, local_sem, send_sem, recv_z, recv_y, recv_c, \
+        x_ref, floc_ref, m_ref, sel_ref, out_ref, fout_ref, G, f_ref, acc, local_sem, send_sem, recv_z, recv_y, recv_c, \
             recv_x = refs
     else:
         x_ref, f_ref, m_ref = refs[:3]
@@ -207,7 +207,7 @@
     for cp in sends:
         cp.wait_send()
     if mode == "first":
-        out_ref[...] = acc[...]
+        out_ref[...] = jnp.where(sel_ref[...] > 0.5, acc[...], 0.0)
     else:
         for ref, value in zip(out_refs, epilogue(acc[...], *[e[...] for e in extra_refs])):
             ref[...] = value
@@ -227,14 +227,14 @@
     return [pl.BlockSpec(memory_space=pltpu.VMEM)] * n
 
 
-def first_product(floc, mask_row, x, cid):
+def first_product(floc, mask_row, sel, x, cid):
     nb, w = x.shape
     rows = floc.shape[0]
     ncol = floc.shape[1] * 4
     return pl.pallas_call(
         functools.partial(gather_kernel, mode="first"),
         out_shape=(jax.ShapeDtypeStruct((rows, w), jnp.float32), jax.ShapeDtypeStruct((rows, ncol), floc.dtype)),
-        in_specs=_specs(3),
+        in_specs=_specs(4),
         out_specs=(pl.BlockSpec(memory_space=pltpu.VMEM), pl.BlockSpec(memory_space=pl.ANY)),
         scratch_shapes=[pltpu.VMEM((NY * NZ, NC, nb, w), x.dtype), pltpu.VMEM((rows, ncol), floc.dtype),
                         pltpu.VMEM((rows, w), jnp.float32)]
@@ -243,7 +243,7 @@
         cost_estimate=pl.CostEstimate(
             flops=2 * rows * ncol * w, transcendentals=0, bytes_accessed=(2 * rows * ncol + 2 * x.size * 64) * 4,
         ),
-    )(x, floc, mask_row)
+    )(x, floc, mask_row, sel)
 
 
 def gather_product(matrix, mask_row, x, cid, extras, epilogue, n_out):
@@ -270,6 +270,11 @@
     return accum, rhs - accum
 
 
+def _first_link_epilogue(prod, rhs):
+    accum = jnp.zeros_like(prod) + prod
+    return accum, rhs - accum
+
+
 def _diag_epilogue(prod, sel, result):
     solved = jnp.where(sel > 0.5, prod, 0.0)
     return solved, result + solved
@@ -280,15 +285,15 @@
     same_row = jnp.repeat(same.astype(jnp.float32), B)[None, :]
     link_row = jnp.repeat(link.astype(jnp.float32), B)[None, :]
 
-    rows0 = level_mine == 0
-    first_prod, full_rows = first_product(factor, same_row, rhs, 0)
-    solved = jnp.where(rows0, first_prod, 0.0)
+    def selector(section):
+        return jnp.full((1, rhs.shape[1]), (level_mine == section).astype(jnp.float32))
+
+    solved, full_rows = first_product(factor, same_row, selector(0), rhs, 0)
     result = solved
-    accum = jnp.zeros(rhs.shape, jnp.float32)
-    accum, vector = gather_product(full_rows, link_row, solved, 1, (accum, rhs), _link_epilogue, 2)
+    accum, vector = gather_product(full_rows, link_row, solved, 1, (rhs,), _first_link_epilogue, 2)
     for section in (1, 2):
-        sel = jnp.full((1, rhs.shape[1]), (level_mine == section).astype(jnp.float32))
-        solved, result = gather_product(full_rows, same_row, vector, 2 * section, (sel, result), _diag_epilogue, 2)
+        solved, result = gather_product(full_rows, same_row, vector, 2 * section, (selector(section), result),
+                                        _diag_epilogue, 2)
         if section < 2:
             accum, vector = gather_product(full_rows, link_row, solved, 2 * section + 1, (accum, rhs),
                                            _link_epilogue, 2)

time: 193 us -> 193 us (level)
  no operation moved by 1% of the time
where the time goes in v8:
time: 193 us; the launch traced here: 192 us
  Pallas kernels  181 us (94%)
  local copies, waits for them, and re-layouts  5.26 us (3%)
  other arithmetic  5.04 us (3%)
    pallas_call x4, Pallas kernels, gather_product(): pl.pallas_call(functools.partial(gather_kernel, mode='fused', epilogue=ep...  131 us
    pallas_call x1, Pallas kernels, first_product(): pl.pallas_call(functools.partial(gather_kernel, mode='first'), out_shape=...  49.4 us

profile of v8, /device:TPU:1, one launch (start us, length us, event | category | flops | bytes accessed | tf_op | source)
XLA Modules:
  0.0 192.3 jit_solution(5580203481838605866)
XLA Ops:
  0.0 0.7 select_reduce_fusion
  0.7 0.7 slice.3
  1.5 0.1 convert_reduce_fusion
  1.6 0.7 fusion
  3.5 0.5 broadcast_in_dim.83.refs_3_
  4.1 0.6 broadcast_in_dim.90.refs_3_
  4.7 0.6 broadcast_in_dim.91.refs_3_
  5.2 0.6 iota_compare_fusion.3
  5.8 0.8 select_reduce_fusion.2
  6.7 0.7 select_reduce_fusion.4
  7.4 0.7 select_reduce_fusion.3
  8.1 0.6 and_convert_fusion
  8.8 0.7 broadcast_in_dim.89
  9.5 0.7 broadcast_in_dim.82
  10.2 49.4 %shard_map.64 = (f32[128,128]{1,0:T(8,128)}, f32[128,8192]{1,0:T(8,128)}) custom-call(f32[128,128]{1,0:T(8,128)} %refs_4_.1, f32[128,2048]{1,0:T(8,128)} %refs_1_.1, f32[1,8192]{1,0:T(1,128)} %bitcast.2, f32[1,128]{1,0:T(1,128)} %broadcast_in_dim.83.refs_3_), custom_call_target="tpu_custom_call" | custom-call | flops 268435456 | bytes 16777216 | tf_op jit(solution)/shard_map/pallas_call | solution.py:234
  59.6 33.1 %shard_map.65 = (f32[128,128]{1,0:T(8,128)}, f32[128,128]{1,0:T(8,128)}) custom-call(f32[128,128]{1,0:T(8,128)} %get-tuple-element.13.refs_0_.refs_4_, f32[128,8192]{1,0:T(8,128)} %get-tuple-element.14.refs_1_, f32[1,8192]{1,0:T(1,128)} %bitcast.5, f32[128,128]{1,0:T(8,128)} %refs_4_.1), custom_call_target="tpu_custom_call" | custom-call | flops 268435456 | bytes 12582912 | tf_op jit(solution)/shard_map/pallas_call | solution.py:253
  92.7 33.1 %shard_map.66 = (f32[128,128]{1,0:T(8,128)}, f32[128,128]{1,0:T(8,128)}) custom-call(f32[128,128]{1,0:T(8,128)} %get-tuple-element.15.refs_0_, f32[128,8192]{1,0:T(8,128)} %get-tuple-element.14.refs_1_, f32[1,8192]{1,0:T(1,128)} %bitcast.3, f32[1,128]{1,0:T(1,128)} %broadcast_in_dim.90.refs_3_, f32[128,128]{1,0:T(8,128)} %get-tuple-element.13.refs_0_.refs_4_), custom_call_target="tpu_custom_call" | custom-call | flops 268435456 | bytes 12582912 | tf_op jit(solution)/shard_map/pallas_call | solution.py:253
  125.8 32.3 %shard_map.67 = (f32[128,128]{1,0:T(8,128)}, f32[128,128]{1,0:T(8,128)}) custom-call(f32[128,128]{1,0:T(8,128)} %get-tuple-element.16.refs_0_, f32[128,8192]{1,0:T(8,128)} %get-tuple-element.14.refs_1_, f32[1,8192]{1,0:T(1,128)} %bitcast.6, f32[128,128]{1,0:T(8,128)} %get-tuple-element.17.refs_3_, f32[128,128]{1,0:T(8,128)} %refs_4_.1), custom_call_target="tpu_custom_call" | custom-call | flops 268435456 | bytes 12582912 | tf_op jit(solution)/shard_map/pallas_call | solution.py:253
  158.1 32.7 %shard_map.68 = (f32[128,128]{1,0:T(8,128)}, f32[128,128]{1,0:T(8,128)}) custom-call(f32[128,128]{1,0:T(8,128)} %get-tuple-element.18.refs_0_, f32[128,8192]{1,0:T(8,128)} %get-tuple-element.14.refs_1_, f32[1,8192]{1,0:T(1,128)} %bitcast.4, f32[1,128]{1,0:T(1,128)} %broadcast_in_dim.91.refs_3_, f32[128,128]{1,0:T(8,128)} %get-tuple-element.19.refs_4_), custom_call_target="tpu_custom_call" | custom-call | flops 268435456 | bytes 12582912 | tf_op jit(solution)/shard_map/pallas_call | solution.py:253
  190.8 1.5 copy.8

commit v9 on v8

--- a/solution.py
+++ b/solution.py
@@ -32,7 +32,7 @@
     return level_r, node == node_r, ancestor & listed
 
 
-def gather_kernel(*refs, mode, epilogue=None, n_extra=0, n_out=1):
+def gather_kernel(*refs, mode, which, section=0, epilogue=None, n_extra=0, n_out=1):
     fused = True
     if mode == "first":
         x_ref, floc_ref, m_ref, sel_ref, out_ref, fout_ref, G, f_ref, acc, local_sem, send_sem, recv_z, recv_y, recv_c, \
@@ -117,7 +117,7 @@
             cols = pl.ds(pl.multiple_of(plane * (NZ * NC * nb), nb), NZ * NC * nb)
             vec = G[pl.ds(plane * NZ, NZ)].reshape(NZ * NC * nb, w)
             acc[...] += jnp.dot(
-                f_ref[:, cols] * m_ref[:, cols], vec,
+                f_ref[:, cols] * m_ref[which:which + 1, cols], vec,
                 precision=lax.Precision.HIGHEST, preferred_element_type=jnp.float32,
             )
 
@@ -207,7 +207,7 @@
     for cp in sends:
         cp.wait_send()
     if mode == "first":
-        out_ref[...] = jnp.where(sel_ref[...] > 0.5, acc[...], 0.0)
+        out_ref[...] = jnp.where(sel_ref[section:section + 1, :] > 0.5, acc[...], 0.0)
     else:
         for ref, value in zip(out_refs, epilogue(acc[...], *[e[...] for e in extra_refs])):
             ref[...] = value
@@ -232,7 +232,7 @@
     rows = floc.shape[0]
     ncol = floc.shape[1] * 4
     return pl.pallas_call(
-        functools.partial(gather_kernel, mode="first"),
+        functools.partial(gather_kernel, mode="first", which=0),
         out_shape=(jax.ShapeDtypeStruct((rows, w), jnp.float32), jax.ShapeDtypeStruct((rows, ncol), floc.dtype)),
         in_specs=_specs(4),
         out_specs=(pl.BlockSpec(memory_space=pltpu.VMEM), pl.BlockSpec(memory_space=pl.ANY)),
@@ -246,12 +246,13 @@
     )(x, floc, mask_row, sel)
 
 
-def gather_product(matrix, mask_row, x, cid, extras, epilogue, n_out):
+def gather_product(matrix, mask_row, which, x, cid, extras, epilogue, n_out):
     nb, w = x.shape
     shape = (NY * NZ, NC, nb, w)
     out = jax.ShapeDtypeStruct((matrix.shape[0], w), jnp.float32)
     return pl.pallas_call(
-        functools.partial(gather_kernel, mode="fused", epilogue=epilogue, n_extra=len(extras), n_out=n_out),
+        functools.partial(gather_kernel, mode="fused", which=which, epilogue=epilogue, n_extra=len(extras),
+                          n_out=n_out),
         out_shape=tuple([out] * n_out),
         in_specs=_specs(3 + len(extras)),
         out_specs=tuple(pl.BlockSpec(memory_space=pltpu.VMEM) for _ in range(n_out)),
@@ -275,27 +276,25 @@
     return accum, rhs - accum
 
 
-def _diag_epilogue(prod, sel, result):
-    solved = jnp.where(sel > 0.5, prod, 0.0)
+def _diag_epilogue(prod, sel, result, section):
+    solved = jnp.where(sel[section:section + 1, :] > 0.5, prod, 0.0)
     return solved, result + solved
 
 
 def body(factor, rhs, parent, bounds, slot, structure):
     level_mine, same, link = row_masks(parent, bounds, slot, structure, lax.axis_index("row"))
-    same_row = jnp.repeat(same.astype(jnp.float32), B)[None, :]
-    link_row = jnp.repeat(link.astype(jnp.float32), B)[None, :]
-
-    def selector(section):
-        return jnp.full((1, rhs.shape[1]), (level_mine == section).astype(jnp.float32))
-
-    solved, full_rows = first_product(factor, same_row, selector(0), rhs, 0)
+    masks = jnp.repeat(jnp.stack([same, link]).astype(jnp.float32), B, axis=1)
+    sels = jnp.repeat((level_mine == jnp.arange(3, dtype=jnp.int32)).astype(jnp.float32)[:, None], rhs.shape[1],
+                      axis=1)
+
+    solved, full_rows = first_product(factor, masks, sels, rhs, 0)
     result = solved
-    accum, vector = gather_product(full_rows, link_row, solved, 1, (rhs,), _first_link_epilogue, 2)
+    accum, vector = gather_product(full_rows, masks, 1, solved, 1, (rhs,), _first_link_epilogue, 2)
     for section in (1, 2):
-        solved, result = gather_product(full_rows, same_row, vector, 2 * section, (selector(section), result),
-                                        _diag_epilogue, 2)
+        epi = functools.partial(_diag_epilogue, section=section)
+        solved, result = gather_product(full_rows, masks, 0, vector, 2 * section, (sels, result), epi, 2)
         if section < 2:
-            accum, vector = gather_product(full_rows, link_row, solved, 2 * section + 1, (accum, rhs),
+            accum, vector = gather_product(full_rows, masks, 1, solved, 2 * section + 1, (accum, rhs),
                                            _link_epilogue, 2)
     return result
 

time: 193 us -> 191 us (0.990)
    broadcast_in_dim x5 -> x0, local copies, waits for them, and re-layouts: 3.05 us -> none  [the longest x3 1.69 us: selector(): jnp.full((1, rhs.shape[1]), (level_mine == section).astype(jnp.float32))]
where the time goes in v9:
time: 191 us
  Pallas kernels  180 us (94%)
  other arithmetic  5.19 us (3%)
  local copies, waits for them, and re-layouts  3.61 us (2%)
    pallas_call x4, Pallas kernels, gather_product(): pl.pallas_call(functools.partial(gather_kernel, mode='fused', which=which...  131 us
    pallas_call x1, Pallas kernels, first_product(): pl.pallas_call(functools.partial(gather_kernel, mode='first', which=0), o...  49.4 us

profile of v9, /device:TPU:1, one launch (start us, length us, event | category | flops | bytes accessed | tf_op | source)
XLA Modules:
  0.0 190.6 jit_solution(9950842876552630893)
XLA Ops:
  0.0 0.7 select_reduce_fusion
  0.7 0.7 slice.3
  1.5 0.1 convert_reduce_fusion
  1.6 0.7 fusion
  3.6 0.7 iota_compare_fusion.3
  4.3 0.8 select_reduce_fusion.2
  5.1 0.7 select_reduce_fusion.4
  5.8 0.7 select_reduce_fusion.3
  6.6 0.7 compare_bitcast_fusion
  7.3 0.6 reshape.76.refs_3_
  7.9 0.1 broadcast_bitcast_fusion
  8.0 0.7 copy.9
  8.7 49.4 %shard_map.64 = (f32[128,128]{1,0:T(8,128)}, f32[128,8192]{1,0:T(8,128)}) custom-call(f32[128,128]{1,0:T(8,128)} %refs_4_.1, f32[128,2048]{1,0:T(8,128)} %refs_1_.1, f32[2,8192]{1,0:T(2,128)} %bitcast.9, f32[3,128]{1,0:T(4,128)} %reshape.76.refs_3_), custom_call_target="tpu_custom_call" | custom-call | flops 268435456 | bytes 16777216 | tf_op jit(solution)/shard_map/pallas_call | solution.py:234
  58.1 33.1 %shard_map.65 = (f32[128,128]{1,0:T(8,128)}, f32[128,128]{1,0:T(8,128)}) custom-call(f32[128,128]{1,0:T(8,128)} %get-tuple-element.13.refs_0_.refs_4_, f32[128,8192]{1,0:T(8,128)} %get-tuple-element.14.refs_1_, f32[2,8192]{1,0:T(2,128)} %bitcast.10, f32[128,128]{1,0:T(8,128)} %refs_4_.1), custom_call_target="tpu_custom_call" | custom-call | flops 268435456 | bytes 12582912 | tf_op jit(solution)/shard_map/pallas_call | solution.py:253
  91.3 32.6 %shard_map.66 = (f32[128,128]{1,0:T(8,128)}, f32[128,128]{1,0:T(8,128)}) custom-call(f32[128,128]{1,0:T(8,128)} %get-tuple-element.15.refs_0_, f32[128,8192]{1,0:T(8,128)} %get-tuple-element.14.refs_1_, f32[2,8192]{1,0:T(2,128)} %bitcast.11, f32[3,128]{1,0:T(4,128)} %reshape.76.refs_3_, f32[128,128]{1,0:T(8,128)} %get-tuple-element.13.refs_0_.refs_4_), custom_call_target="tpu_custom_call" | custom-call | flops 268435456 | bytes 12582912 | tf_op jit(solution)/shard_map/pallas_call | solution.py:253
  123.8 32.5 %shard_map.67 = (f32[128,128]{1,0:T(8,128)}, f32[128,128]{1,0:T(8,128)}) custom-call(f32[128,128]{1,0:T(8,128)} %get-tuple-element.16.refs_0_, f32[128,8192]{1,0:T(8,128)} %get-tuple-element.14.refs_1_, f32[2,8192]{1,0:T(2,128)} %bitcast.12, f32[128,128]{1,0:T(8,128)} %get-tuple-element.17.refs_3_, f32[128,128]{1,0:T(8,128)} %refs_4_.1), custom_call_target="tpu_custom_call" | custom-call | flops 268435456 | bytes 12582912 | tf_op jit(solution)/shard_map/pallas_call | solution.py:253
  156.3 32.7 %shard_map.68 = (f32[128,128]{1,0:T(8,128)}, f32[128,128]{1,0:T(8,128)}) custom-call(f32[128,128]{1,0:T(8,128)} %get-tuple-element.18.refs_0_, f32[128,8192]{1,0:T(8,128)} %get-tuple-element.14.refs_1_, f32[2,8192]{1,0:T(2,128)} %bitcast.13, f32[3,128]{1,0:T(4,128)} %reshape.76.refs_3_, f32[128,128]{1,0:T(8,128)} %get-tuple-element.19.refs_4_), custom_call_target="tpu_custom_call" | custom-call | flops 268435456 | bytes 12582912 | tf_op jit(solution)/shard_map/pallas_call | solution.py:253
  189.1 1.5 copy.11
  (2 shorter events, 0.0 us)

commit v10 on v9

--- a/solution.py
+++ b/solution.py
@@ -276,6 +276,10 @@
     return accum, rhs - accum
 
 
+def _last_epilogue(prod, sel):
+    return (jnp.where(sel[2:3, :] > 0.5, prod, 0.0),)
+
+
 def _diag_epilogue(prod, sel, result, section):
     solved = jnp.where(sel[section:section + 1, :] > 0.5, prod, 0.0)
     return solved, result + solved
@@ -290,13 +294,11 @@
     solved, full_rows = first_product(factor, masks, sels, rhs, 0)
     result = solved
     accum, vector = gather_product(full_rows, masks, 1, solved, 1, (rhs,), _first_link_epilogue, 2)
-    for section in (1, 2):
-        epi = functools.partial(_diag_epilogue, section=section)
-        solved, result = gather_product(full_rows, masks, 0, vector, 2 * section, (sels, result), epi, 2)
-        if section < 2:
-            accum, vector = gather_product(full_rows, masks, 1, solved, 2 * section + 1, (accum, rhs),
-                                           _link_epilogue, 2)
-    return result
+    epi = functools.partial(_diag_epilogue, section=1)
+    solved, result = gather_product(full_rows, masks, 0, vector, 2, (sels, result), epi, 2)
+    accum, vector = gather_product(full_rows, masks, 1, solved, 3, (accum, rhs), _link_epilogue, 2)
+    (solved,) = gather_product(full_rows, masks, 0, vector, 4, (sels,), _last_epilogue, 1)
+    return result + solved
 
 
 def solution(mesh):

time: 191 us -> 191 us (level)
  no operation moved by 1% of the time
where the time goes in v10:
time: 191 us
  Pallas kernels  180 us (94%)
  other arithmetic  6.67 us (3%)
  local copies, waits for them, and re-layouts  2.14 us (1%)
    pallas_call x4, Pallas kernels, gather_product(): pl.pallas_call(functools.partial(gather_kernel, mode='fused', which=which...  131 us
    pallas_call x1, Pallas kernels, first_product(): pl.pallas_call(functools.partial(gather_kernel, mode='first', which=0), o...  49.4 us

profile of v10, /device:TPU:1, one launch (start us, length us, event | category | flops | bytes accessed | tf_op | source)
XLA Modules:
  0.0 190.7 jit_solution(7079762882383925244)
XLA Ops:
  0.0 0.7 select_reduce_fusion
  0.7 0.7 slice.3
  1.5 0.1 convert_reduce_fusion
  1.6 0.7 fusion
  3.6 0.7 iota_compare_fusion.3
  4.3 0.8 select_reduce_fusion.2
  5.1 0.7 select_reduce_fusion.4
  5.8 0.7 select_reduce_fusion.3
  6.6 0.7 compare_bitcast_fusion
  7.3 0.6 reshape.76.refs_3_
  7.9 0.1 broadcast_bitcast_fusion
  8.0 0.7 copy.9
  8.7 49.4 %shard_map.64 = (f32[128,128]{1,0:T(8,128)}, f32[128,8192]{1,0:T(8,128)}) custom-call(f32[128,128]{1,0:T(8,128)} %refs_4_.1, f32[128,2048]{1,0:T(8,128)} %refs_1_.1, f32[2,8192]{1,0:T(2,128)} %bitcast.9, f32[3,128]{1,0:T(4,128)} %reshape.76.refs_3_), custom_call_target="tpu_custom_call" | custom-call | flops 268435456 | bytes 16777216 | tf_op jit(solution)/shard_map/pallas_call | solution.py:234
  58.1 33.1 %shard_map.65 = (f32[128,128]{1,0:T(8,128)}, f32[128,128]{1,0:T(8,128)}) custom-call(f32[128,128]{1,0:T(8,128)} %get-tuple-element.12.refs_0_.refs_4_, f32[128,8192]{1,0:T(8,128)} %get-tuple-element.13.refs_1_, f32[2,8192]{1,0:T(2,128)} %bitcast.10, f32[128,128]{1,0:T(8,128)} %refs_4_.1), custom_call_target="tpu_custom_call" | custom-call | flops 268435456 | bytes 12582912 | tf_op jit(solution)/shard_map/pallas_call | solution.py:253
  91.3 32.6 %shard_map.66 = (f32[128,128]{1,0:T(8,128)}, f32[128,128]{1,0:T(8,128)}) custom-call(f32[128,128]{1,0:T(8,128)} %get-tuple-element.14.refs_0_, f32[128,8192]{1,0:T(8,128)} %get-tuple-element.13.refs_1_, f32[2,8192]{1,0:T(2,128)} %bitcast.11, f32[3,128]{1,0:T(4,128)} %reshape.76.refs_3_, f32[128,128]{1,0:T(8,128)} %get-tuple-element.12.refs_0_.refs_4_), custom_call_target="tpu_custom_call" | custom-call | flops 268435456 | bytes 12582912 | tf_op jit(solution)/shard_map/pallas_call | solution.py:253
  123.9 0.0 copy-start
  123.9 32.5 %shard_map.67 = (f32[128,128]{1,0:T(8,128)}, f32[128,128]{1,0:T(8,128)}) custom-call(f32[128,128]{1,0:T(8,128)} %get-tuple-element.16.refs_0_, f32[128,8192]{1,0:T(8,128)} %get-tuple-element.13.refs_1_, f32[2,8192]{1,0:T(2,128)} %bitcast.12, f32[128,128]{1,0:T(8,128)} %get-tuple-element.17.refs_3_, f32[128,128]{1,0:T(8,128)} %refs_4_.1), custom_call_target="tpu_custom_call" | custom-call | flops 268435456 | bytes 12582912 | tf_op jit(solution)/shard_map/pallas_call | solution.py:253
  156.4 32.8 %shard_map.68 = f32[128,128]{1,0:T(8,128)} custom-call(f32[128,128]{1,0:T(8,128)} %get-tuple-element.18.refs_0_, f32[128,8192]{1,0:T(8,128)} %get-tuple-element.13.refs_1_, f32[2,8192]{1,0:T(2,128)} %bitcast.13, f32[3,128]{1,0:T(4,128)} %reshape.76.refs_3_), custom_call_target="tpu_custom_call" | custom-call | flops 268435456 | bytes 12582912 | tf_op jit(solution)/shard_map/pallas_call | solution.py:253
  189.2 0.0 copy-done
  189.2 1.5 add.7
  (2 shorter events, 0.0 us)
Async XLA Ops:
  123.9 65.3 %copy-start = (f32[128,128]{1,0:T(8,128)S(1)}, f32[128,128]{1,0:T(8,128)}, u32[]{:S(2)}) copy-start(f32[128,128]{1,0:T(8,128)} %get-tuple-element.15) | copy-start | bytes 196612

commit v11 on v10

--- a/solution.py
+++ b/solution.py
@@ -91,7 +91,13 @@
 
         flocal = pltpu.make_async_copy(floc_ref, fcols(c), local_sem.at[1])
         flocal.start()
-        xsends = [xcopy(floc_ref, fcols(c), 64, recv_x.at[0], xr), xcopy(floc_ref, fcols(c), 65, recv_x.at[1], xl)]
+        lo_half, hi_half = floc_ref.at[:, pl.ds(0, hcol)], floc_ref.at[:, pl.ds(hcol, hcol)]
+        xsends = [
+            xcopy(lo_half, fcols(c, 0, hcol), 64, recv_x.at[0], xr),
+            xcopy(hi_half, fcols(c, hcol, hcol), 65, recv_x.at[1], xl),
+            xcopy(hi_half, fcols(c, hcol, hcol), 68, recv_x.at[4], xr),
+            xcopy(lo_half, fcols(c, 0, hcol), 69, recv_x.at[5], xl),
+        ]
         for cp in xsends:
             cp.start()
 
@@ -172,10 +178,10 @@
             wait(blk(y + d, z + off, 1 - k), recv_c.at[d % NY, i])
 
     if mode == "first":
-        xcopy(floc_ref, fcols(c - 1), 0, recv_x.at[0], xr).wait_recv()
+        xcopy(lo_half, fcols(c - 1, 0, hcol), 0, recv_x.at[0], xr).wait_recv()
         xsends.append(xcopy(fcols(c - 1, 0, hcol), fcols(c - 1, 0, hcol), 66, recv_x.at[2], xr))
         xsends[-1].start()
-        xcopy(floc_ref, fcols(c + 1), 0, recv_x.at[1], xr).wait_recv()
+        xcopy(hi_half, fcols(c + 1, hcol, hcol), 0, recv_x.at[1], xr).wait_recv()
         xsends.append(xcopy(fcols(c + 1, hcol, hcol), fcols(c + 1, hcol, hcol), 67, recv_x.at[3], xl))
         xsends[-1].start()
     else:
@@ -189,7 +195,9 @@
             partner_wait(d)
         flocal.wait()
         multiply(c)
+        xcopy(hi_half, fcols(c - 1, hcol, hcol), 0, recv_x.at[4], xr).wait_recv()
         multiply(c - 1)
+        xcopy(lo_half, fcols(c + 1, 0, hcol), 0, recv_x.at[5], xr).wait_recv()
         multiply(c + 1)
         xcopy(fcols(c + 2, 0, hcol), fcols(c + 2, 0, hcol), 0, recv_x.at[2], xr).wait_recv()
         xcopy(fcols(c + 2, hcol, hcol), fcols(c + 2, hcol, hcol), 0, recv_x.at[3], xr).wait_recv()
@@ -216,7 +224,7 @@
 def _sems():
     return [
         pltpu.SemaphoreType.DMA((2,)),
-        pltpu.SemaphoreType.DMA((68,)),
+        pltpu.SemaphoreType.DMA((70,)),
         pltpu.SemaphoreType.DMA((NZ,)),
         pltpu.SemaphoreType.DMA((4, NZ)),
         pltpu.SemaphoreType.DMA((NY, NZ)),
@@ -238,7 +246,7 @@
         out_specs=(pl.BlockSpec(memory_space=pltpu.VMEM), pl.BlockSpec(memory_space=pl.ANY)),
         scratch_shapes=[pltpu.VMEM((NY * NZ, NC, nb, w), x.dtype), pltpu.VMEM((rows, ncol), floc.dtype),
                         pltpu.VMEM((rows, w), jnp.float32)]
-        + _sems() + [pltpu.SemaphoreType.DMA((4,))],
+        + _sems() + [pltpu.SemaphoreType.DMA((6,))],
         compiler_params=pltpu.CompilerParams(collective_id=cid, has_side_effects=True),
         cost_estimate=pl.CostEstimate(
             flops=2 * rows * ncol * w, transcendentals=0, bytes_accessed=(2 * rows * ncol + 2 * x.size * 64) * 4,

time: 191 us -> 190 us (level)
  no operation moved by 1% of the time
where the time goes in v11:
time: 190 us
  Pallas kernels  180 us (95%)
  other arithmetic  6.67 us (4%)
  local copies, waits for them, and re-layouts  2.14 us (1%)
    pallas_call x4, Pallas kernels, gather_product(): pl.pallas_call(functools.partial(gather_kernel, mode='fused', which=which...  130 us
    pallas_call x1, Pallas kernels, first_product(): pl.pallas_call(functools.partial(gather_kernel, mode='first', which=0), o...  49.5 us

profile of v11, /device:TPU:1, one launch (start us, length us, event | category | flops | bytes accessed | tf_op | source)
XLA Modules:
  0.0 190.2 jit_solution(4472447196399810297)
XLA Ops:
  0.0 0.7 select_reduce_fusion
  0.7 0.7 slice.3
  1.5 0.1 convert_reduce_fusion
  1.6 0.7 fusion
  3.6 0.7 iota_compare_fusion.3
  4.3 0.8 select_reduce_fusion.2
  5.1 0.7 select_reduce_fusion.4
  5.8 0.7 select_reduce_fusion.3
  6.6 0.7 compare_bitcast_fusion
  7.3 0.6 reshape.76.refs_3_
  7.9 0.1 broadcast_bitcast_fusion
  8.0 0.7 copy.9
  8.7 49.5 %shard_map.64 = (f32[128,128]{1,0:T(8,128)}, f32[128,8192]{1,0:T(8,128)}) custom-call(f32[128,128]{1,0:T(8,128)} %refs_4_.1, f32[128,2048]{1,0:T(8,128)} %refs_1_.1, f32[2,8192]{1,0:T(2,128)} %bitcast.9, f32[3,128]{1,0:T(4,128)} %reshape.76.refs_3_), custom_call_target="tpu_custom_call" | custom-call | flops 268435456 | bytes 16777216 | tf_op jit(solution)/shard_map/pallas_call | solution.py:242
  58.2 32.8 %shard_map.65 = (f32[128,128]{1,0:T(8,128)}, f32[128,128]{1,0:T(8,128)}) custom-call(f32[128,128]{1,0:T(8,128)} %get-tuple-element.12.refs_0_.refs_4_, f32[128,8192]{1,0:T(8,128)} %get-tuple-element.13.refs_1_, f32[2,8192]{1,0:T(2,128)} %bitcast.10, f32[128,128]{1,0:T(8,128)} %refs_4_.1), custom_call_target="tpu_custom_call" | custom-call | flops 268435456 | bytes 12582912 | tf_op jit(solution)/shard_map/pallas_call | solution.py:261
  91.0 32.9 %shard_map.66 = (f32[128,128]{1,0:T(8,128)}, f32[128,128]{1,0:T(8,128)}) custom-call(f32[128,128]{1,0:T(8,128)} %get-tuple-element.14.refs_0_, f32[128,8192]{1,0:T(8,128)} %get-tuple-element.13.refs_1_, f32[2,8192]{1,0:T(2,128)} %bitcast.11, f32[3,128]{1,0:T(4,128)} %reshape.76.refs_3_, f32[128,128]{1,0:T(8,128)} %get-tuple-element.12.refs_0_.refs_4_), custom_call_target="tpu_custom_call" | custom-call | flops 268435456 | bytes 12582912 | tf_op jit(solution)/shard_map/pallas_call | solution.py:261
  123.9 0.0 copy-start
  123.9 32.5 %shard_map.67 = (f32[128,128]{1,0:T(8,128)}, f32[128,128]{1,0:T(8,128)}) custom-call(f32[128,128]{1,0:T(8,128)} %get-tuple-element.16.refs_0_, f32[128,8192]{1,0:T(8,128)} %get-tuple-element.13.refs_1_, f32[2,8192]{1,0:T(2,128)} %bitcast.12, f32[128,128]{1,0:T(8,128)} %get-tuple-element.17.refs_3_, f32[128,128]{1,0:T(8,128)} %refs_4_.1), custom_call_target="tpu_custom_call" | custom-call | flops 268435456 | bytes 12582912 | tf_op jit(solution)/shard_map/pallas_call | solution.py:261
  156.5 32.2 %shard_map.68 = f32[128,128]{1,0:T(8,128)} custom-call(f32[128,128]{1,0:T(8,128)} %get-tuple-element.18.refs_0_, f32[128,8192]{1,0:T(8,128)} %get-tuple-element.13.refs_1_, f32[2,8192]{1,0:T(2,128)} %bitcast.13, f32[3,128]{1,0:T(4,128)} %reshape.76.refs_3_), custom_call_target="tpu_custom_call" | custom-call | flops 268435456 | bytes 12582912 | tf_op jit(solution)/shard_map/pallas_call | solution.py:261
  188.7 0.0 copy-done
  188.7 1.5 add.7
  (2 shorter events, 0.0 us)
Async XLA Ops:
  123.9 64.8 %copy-start = (f32[128,128]{1,0:T(8,128)S(1)}, f32[128,128]{1,0:T(8,128)}, u32[]{:S(2)}) copy-start(f32[128,128]{1,0:T(8,128)} %get-tuple-element.15) | copy-start | bytes 196612

commit v12 on v10

--- a/solution.py
+++ b/solution.py
@@ -178,9 +178,6 @@
         xcopy(floc_ref, fcols(c + 1), 0, recv_x.at[1], xr).wait_recv()
         xsends.append(xcopy(fcols(c + 1, hcol, hcol), fcols(c + 1, hcol, hcol), 67, recv_x.at[3], xl))
         xsends[-1].start()
-    else:
-        partner_wait(0)
-        multiply(y)
     for i, off in enumerate(offs):
         wait(blk(y + 2, z + off, k), recv_y.at[2 if off in to_right else 3, i])
         send(blk(y + 2, z + off, k), blk(y + 2, z + off, k), recv_c.at[2, i], partner)
@@ -200,7 +197,7 @@
         fout.start()
         fout.wait()
     else:
-        for d in (-1, 1, 2):
+        for d in (0, -1, 1, 2):
             partner_wait(d)
             multiply(y + d)
 

time: 191 us -> 193 us (1.010)
  Pallas kernels: 180 us -> 182 us
where the time goes in v12:
time: 193 us
  Pallas kernels  182 us (94%)
  other arithmetic  6.67 us (3%)
  local copies, waits for them, and re-layouts  2.14 us (1%)
    pallas_call x4, Pallas kernels, gather_product(): pl.pallas_call(functools.partial(gather_kernel, mode='fused', which=which...  133 us
    pallas_call x1, Pallas kernels, first_product(): pl.pallas_call(functools.partial(gather_kernel, mode='first', which=0), o...  49.4 us

profile of v12, /device:TPU:1, one launch (start us, length us, event | category | flops | bytes accessed | tf_op | source)
XLA Modules:
  0.0 192.6 jit_solution(12043223927146274848)
XLA Ops:
  0.0 0.7 select_reduce_fusion
  0.7 0.7 slice.3
  1.5 0.1 convert_reduce_fusion
  1.6 0.7 fusion
  3.6 0.7 iota_compare_fusion.3
  4.3 0.8 select_reduce_fusion.2
  5.1 0.7 select_reduce_fusion.4
  5.8 0.7 select_reduce_fusion.3
  6.6 0.7 compare_bitcast_fusion
  7.3 0.6 reshape.76.refs_3_
  7.9 0.1 broadcast_bitcast_fusion
  8.0 0.7 copy.9
  8.7 49.4 %shard_map.64 = (f32[128,128]{1,0:T(8,128)}, f32[128,8192]{1,0:T(8,128)}) custom-call(f32[128,128]{1,0:T(8,128)} %refs_4_.1, f32[128,2048]{1,0:T(8,128)} %refs_1_.1, f32[2,8192]{1,0:T(2,128)} %bitcast.9, f32[3,128]{1,0:T(4,128)} %reshape.76.refs_3_), custom_call_target="tpu_custom_call" | custom-call | flops 268435456 | bytes 16777216 | tf_op jit(solution)/shard_map/pallas_call | solution.py:231
  58.1 33.1 %shard_map.65 = (f32[128,128]{1,0:T(8,128)}, f32[128,128]{1,0:T(8,128)}) custom-call(f32[128,128]{1,0:T(8,128)} %get-tuple-element.12.refs_0_.refs_4_, f32[128,8192]{1,0:T(8,128)} %get-tuple-element.13.refs_1_, f32[2,8192]{1,0:T(2,128)} %bitcast.10, f32[128,128]{1,0:T(8,128)} %refs_4_.1), custom_call_target="tpu_custom_call" | custom-call | flops 268435456 | bytes 12582912 | tf_op jit(solution)/shard_map/pallas_call | solution.py:250
  91.3 33.3 %shard_map.66 = (f32[128,128]{1,0:T(8,128)}, f32[128,128]{1,0:T(8,128)}) custom-call(f32[128,128]{1,0:T(8,128)} %get-tuple-element.14.refs_0_, f32[128,8192]{1,0:T(8,128)} %get-tuple-element.13.refs_1_, f32[2,8192]{1,0:T(2,128)} %bitcast.11, f32[3,128]{1,0:T(4,128)} %reshape.76.refs_3_, f32[128,128]{1,0:T(8,128)} %get-tuple-element.12.refs_0_.refs_4_), custom_call_target="tpu_custom_call" | custom-call | flops 268435456 | bytes 12582912 | tf_op jit(solution)/shard_map/pallas_call | solution.py:250
  124.6 0.0 copy-start
  124.6 33.1 %shard_map.67 = (f32[128,128]{1,0:T(8,128)}, f32[128,128]{1,0:T(8,128)}) custom-call(f32[128,128]{1,0:T(8,128)} %get-tuple-element.16.refs_0_, f32[128,8192]{1,0:T(8,128)} %get-tuple-element.13.refs_1_, f32[2,8192]{1,0:T(2,128)} %bitcast.12, f32[128,128]{1,0:T(8,128)} %get-tuple-element.17.refs_3_, f32[128,128]{1,0:T(8,128)} %refs_4_.1), custom_call_target="tpu_custom_call" | custom-call | flops 268435456 | bytes 12582912 | tf_op jit(solution)/shard_map/pallas_call | solution.py:250
  157.7 33.5 %shard_map.68 = f32[128,128]{1,0:T(8,128)} custom-call(f32[128,128]{1,0:T(8,128)} %get-tuple-element.18.refs_0_, f32[128,8192]{1,0:T(8,128)} %get-tuple-element.13.refs_1_, f32[2,8192]{1,0:T(2,128)} %bitcast.13, f32[3,128]{1,0:T(4,128)} %reshape.76.refs_3_), custom_call_target="tpu_custom_call" | custom-call | flops 268435456 | bytes 12582912 | tf_op jit(solution)/shard_map/pallas_call | solution.py:250
  191.1 0.0 copy-done
  191.1 1.5 add.7
  (2 shorter events, 0.0 us)
Async XLA Ops:
  124.6 66.5 %copy-start = (f32[128,128]{1,0:T(8,128)S(1)}, f32[128,128]{1,0:T(8,128)}, u32[]{:S(2)}) copy-start(f32[128,128]{1,0:T(8,128)} %get-tuple-element.15) | copy-start | bytes 196612

commit v13 on v12

--- a/solution.py
+++ b/solution.py
@@ -151,6 +151,10 @@
         wait(blk(y, z + off, k), recv_of(z + off))
         spread(off)
     local.wait()
+    if mode != "first":
+        for i, off in enumerate(offs):
+            wait(blk(y, z + off, 1 - k), recv_c.at[0, i])
+        multiply(y)
 
     for i, off in enumerate(offs):
         wait(blk(y - 1, z + off, k), recv_y.at[0, i])
@@ -197,7 +201,7 @@
         fout.start()
         fout.wait()
     else:
-        for d in (0, -1, 1, 2):
+        for d in (-1, 1, 2):
             partner_wait(d)
             multiply(y + d)
 

time: 193 us -> 190 us (0.984)
  Pallas kernels: 182 us -> 180 us
    pallas_call x4, Pallas kernels: 133 us -> 130 us  [gather_product(): pl.pallas_call(functools.partial(gather_kernel, mode='fused', which=which...]
where the time goes in v13:
time: 190 us
  Pallas kernels  180 us (95%)
  other arithmetic  6.67 us (4%)
  local copies, waits for them, and re-layouts  2.14 us (1%)
    pallas_call x4, Pallas kernels, gather_product(): pl.pallas_call(functools.partial(gather_kernel, mode='fused', which=which...  130 us
    pallas_call x1, Pallas kernels, first_product(): pl.pallas_call(functools.partial(gather_kernel, mode='first', which=0), o...  49.4 us

profile of v13, /device:TPU:1, one launch (start us, length us, event | category | flops | bytes accessed | tf_op | source)
XLA Modules:
  0.0 189.8 jit_solution(12280087039319806579)
XLA Ops:
  0.0 0.7 select_reduce_fusion
  0.7 0.7 slice.3
  1.5 0.1 convert_reduce_fusion
  1.6 0.7 fusion
  3.6 0.7 iota_compare_fusion.3
  4.3 0.8 select_reduce_fusion.2
  5.1 0.7 select_reduce_fusion.4
  5.8 0.7 select_reduce_fusion.3
  6.6 0.7 compare_bitcast_fusion
  7.3 0.6 reshape.76.refs_3_
  7.9 0.1 broadcast_bitcast_fusion
  8.0 0.7 copy.9
  8.7 49.4 %shard_map.64 = (f32[128,128]{1,0:T(8,128)}, f32[128,8192]{1,0:T(8,128)}) custom-call(f32[128,128]{1,0:T(8,128)} %refs_4_.1, f32[128,2048]{1,0:T(8,128)} %refs_1_.1, f32[2,8192]{1,0:T(2,128)} %bitcast.9, f32[3,128]{1,0:T(4,128)} %reshape.76.refs_3_), custom_call_target="tpu_custom_call" | custom-call | flops 268435456 | bytes 16777216 | tf_op jit(solution)/shard_map/pallas_call | solution.py:235
  58.1 33.1 %shard_map.65 = (f32[128,128]{1,0:T(8,128)}, f32[128,128]{1,0:T(8,128)}) custom-call(f32[128,128]{1,0:T(8,128)} %get-tuple-element.12.refs_0_.refs_4_, f32[128,8192]{1,0:T(8,128)} %get-tuple-element.13.refs_1_, f32[2,8192]{1,0:T(2,128)} %bitcast.10, f32[128,128]{1,0:T(8,128)} %refs_4_.1), custom_call_target="tpu_custom_call" | custom-call | flops 268435456 | bytes 12582912 | tf_op jit(solution)/shard_map/pallas_call | solution.py:254
  91.3 31.7 %shard_map.66 = (f32[128,128]{1,0:T(8,128)}, f32[128,128]{1,0:T(8,128)}) custom-call(f32[128,128]{1,0:T(8,128)} %get-tuple-element.14.refs_0_, f32[128,8192]{1,0:T(8,128)} %get-tuple-element.13.refs_1_, f32[2,8192]{1,0:T(2,128)} %bitcast.11, f32[3,128]{1,0:T(4,128)} %reshape.76.refs_3_, f32[128,128]{1,0:T(8,128)} %get-tuple-element.12.refs_0_.refs_4_), custom_call_target="tpu_custom_call" | custom-call | flops 268435456 | bytes 12582912 | tf_op jit(solution)/shard_map/pallas_call | solution.py:254
  122.9 0.0 copy-start
  122.9 32.8 %shard_map.67 = (f32[128,128]{1,0:T(8,128)}, f32[128,128]{1,0:T(8,128)}) custom-call(f32[128,128]{1,0:T(8,128)} %get-tuple-element.16.refs_0_, f32[128,8192]{1,0:T(8,128)} %get-tuple-element.13.refs_1_, f32[2,8192]{1,0:T(2,128)} %bitcast.12, f32[128,128]{1,0:T(8,128)} %get-tuple-element.17.refs_3_, f32[128,128]{1,0:T(8,128)} %refs_4_.1), custom_call_target="tpu_custom_call" | custom-call | flops 268435456 | bytes 12582912 | tf_op jit(solution)/shard_map/pallas_call | solution.py:254
  155.8 32.6 %shard_map.68 = f32[128,128]{1,0:T(8,128)} custom-call(f32[128,128]{1,0:T(8,128)} %get-tuple-element.18.refs_0_, f32[128,8192]{1,0:T(8,128)} %get-tuple-element.13.refs_1_, f32[2,8192]{1,0:T(2,128)} %bitcast.13, f32[3,128]{1,0:T(4,128)} %reshape.76.refs_3_), custom_call_target="tpu_custom_call" | custom-call | flops 268435456 | bytes 12582912 | tf_op jit(solution)/shard_map/pallas_call | solution.py:254
  188.3 0.0 copy-done
  188.4 1.5 add.7
  (2 shorter events, 0.0 us)
Async XLA Ops:
  122.9 65.4 %copy-start = (f32[128,128]{1,0:T(8,128)S(1)}, f32[128,128]{1,0:T(8,128)}, u32[]{:S(2)}) copy-start(f32[128,128]{1,0:T(8,128)} %get-tuple-element.15) | copy-start | bytes 196612

commit v14 on v13

--- a/solution.py
+++ b/solution.py
@@ -182,6 +182,10 @@
         xcopy(floc_ref, fcols(c + 1), 0, recv_x.at[1], xr).wait_recv()
         xsends.append(xcopy(fcols(c + 1, hcol, hcol), fcols(c + 1, hcol, hcol), 67, recv_x.at[3], xl))
         xsends[-1].start()
+    if mode != "first":
+        for d in (-1, 1):
+            partner_wait(d)
+            multiply(y + d)
     for i, off in enumerate(offs):
         wait(blk(y + 2, z + off, k), recv_y.at[2 if off in to_right else 3, i])
         send(blk(y + 2, z + off, k), blk(y + 2, z + off, k), recv_c.at[2, i], partner)
@@ -201,9 +205,8 @@
         fout.start()
         fout.wait()
     else:
-        for d in (-1, 1, 2):
-            partner_wait(d)
-            multiply(y + d)
+        partner_wait(2)
+        multiply(y + 2)
 
     for cp in sends:
         cp.wait_send()

time: 190 us -> 193 us (1.016)
  Pallas kernels: 180 us -> 183 us
    pallas_call x4, Pallas kernels: 130 us -> 133 us  [gather_product(): pl.pallas_call(functools.partial(gather_kernel, mode='fused', which=which...]
where the time goes in v14:
time: 193 us
  Pallas kernels  183 us (95%)
  other arithmetic  6.67 us (3%)
  local copies, waits for them, and re-layouts  2.14 us (1%)
    pallas_call x4, Pallas kernels, gather_product(): pl.pallas_call(functools.partial(gather_kernel, mode='fused', which=which...  133 us
    pallas_call x1, Pallas kernels, first_product(): pl.pallas_call(functools.partial(gather_kernel, mode='first', which=0), o...  49.4 us

profile of v14, /device:TPU:1, one launch (start us, length us, event | category | flops | bytes accessed | tf_op | source)
XLA Modules:
  0.0 192.9 jit_solution(11353978755088427580)
XLA Ops:
  0.0 0.7 select_reduce_fusion
  0.7 0.7 slice.3
  1.5 0.1 convert_reduce_fusion
  1.6 0.7 fusion
  3.6 0.7 iota_compare_fusion.3
  4.3 0.8 select_reduce_fusion.2
  5.1 0.7 select_reduce_fusion.4
  5.8 0.7 select_reduce_fusion.3
  6.6 0.7 compare_bitcast_fusion
  7.3 0.6 reshape.76.refs_3_
  7.9 0.1 broadcast_bitcast_fusion
  8.0 0.7 copy.9
  8.7 49.4 %shard_map.64 = (f32[128,128]{1,0:T(8,128)}, f32[128,8192]{1,0:T(8,128)}) custom-call(f32[128,128]{1,0:T(8,128)} %refs_4_.1, f32[128,2048]{1,0:T(8,128)} %refs_1_.1, f32[2,8192]{1,0:T(2,128)} %bitcast.9, f32[3,128]{1,0:T(4,128)} %reshape.76.refs_3_), custom_call_target="tpu_custom_call" | custom-call | flops 268435456 | bytes 16777216 | tf_op jit(solution)/shard_map/pallas_call | solution.py:238
  58.1 33.1 %shard_map.65 = (f32[128,128]{1,0:T(8,128)}, f32[128,128]{1,0:T(8,128)}) custom-call(f32[128,128]{1,0:T(8,128)} %get-tuple-element.12.refs_0_.refs_4_, f32[128,8192]{1,0:T(8,128)} %get-tuple-element.13.refs_1_, f32[2,8192]{1,0:T(2,128)} %bitcast.10, f32[128,128]{1,0:T(8,128)} %refs_4_.1), custom_call_target="tpu_custom_call" | custom-call | flops 268435456 | bytes 12582912 | tf_op jit(solution)/shard_map/pallas_call | solution.py:257
  91.3 32.6 %shard_map.66 = (f32[128,128]{1,0:T(8,128)}, f32[128,128]{1,0:T(8,128)}) custom-call(f32[128,128]{1,0:T(8,128)} %get-tuple-element.14.refs_0_, f32[128,8192]{1,0:T(8,128)} %get-tuple-element.13.refs_1_, f32[2,8192]{1,0:T(2,128)} %bitcast.11, f32[3,128]{1,0:T(4,128)} %reshape.76.refs_3_, f32[128,128]{1,0:T(8,128)} %get-tuple-element.12.refs_0_.refs_4_), custom_call_target="tpu_custom_call" | custom-call | flops 268435456 | bytes 12582912 | tf_op jit(solution)/shard_map/pallas_call | solution.py:257
  123.9 0.0 copy-start
  123.9 32.9 %shard_map.67 = (f32[128,128]{1,0:T(8,128)}, f32[128,128]{1,0:T(8,128)}) custom-call(f32[128,128]{1,0:T(8,128)} %get-tuple-element.16.refs_0_, f32[128,8192]{1,0:T(8,128)} %get-tuple-element.13.refs_1_, f32[2,8192]{1,0:T(2,128)} %bitcast.12, f32[128,128]{1,0:T(8,128)} %get-tuple-element.17.refs_3_, f32[128,128]{1,0:T(8,128)} %refs_4_.1), custom_call_target="tpu_custom_call" | custom-call | flops 268435456 | bytes 12582912 | tf_op jit(solution)/shard_map/pallas_call | solution.py:257
  156.8 34.6 %shard_map.68 = f32[128,128]{1,0:T(8,128)} custom-call(f32[128,128]{1,0:T(8,128)} %get-tuple-element.18.refs_0_, f32[128,8192]{1,0:T(8,128)} %get-tuple-element.13.refs_1_, f32[2,8192]{1,0:T(2,128)} %bitcast.13, f32[3,128]{1,0:T(4,128)} %reshape.76.refs_3_), custom_call_target="tpu_custom_call" | custom-call | flops 268435456 | bytes 12582912 | tf_op jit(solution)/shard_map/pallas_call | solution.py:257
  191.4 0.0 copy-done
  191.4 1.5 add.7
  (2 shorter events, 0.0 us)
Async XLA Ops:
  123.9 67.5 %copy-start = (f32[128,128]{1,0:T(8,128)S(1)}, f32[128,128]{1,0:T(8,128)}, u32[]{:S(2)}) copy-start(f32[128,128]{1,0:T(8,128)} %get-tuple-element.15) | copy-start | bytes 196612

commit v15 on v13

--- a/solution.py
+++ b/solution.py
@@ -63,7 +63,7 @@
     partner = dev(y, z, 1 - k)
 
     barrier = pltpu.get_barrier_semaphore()
-    peers = [(d, c) for d in (zr, zl, dev(y, z + 2, k), dev(y, z - 2, k), yr, yl, partner)]
+    peers = [(d, c) for d in (zr, zl, yr, yl, partner)]
     nx = 4
     xr, xl = (r, (c + 1) % nx), (r, (c + nx - 1) % nx)
     if mode == "first":
@@ -134,22 +134,24 @@
     def recv_of(zsrc):
         return recv_z.at[(zsrc + NZ) % NZ]
 
-    for d in (1, 2, -1, -2):
-        send(x_ref, blk(y, z, k), recv_of(z), dev(y, z + d, k))
-    spread(0)
-    wait(blk(y, z - 2, k), recv_of(z - 2))
-    send(blk(y, z - 2, k), blk(y, z - 2, k), recv_of(z - 2), dev(y, z + 1, k))
-    send(blk(y, z - 2, k), blk(y, z - 2, k), recv_of(z - 2), dev(y, z + 2, k))
-    wait(blk(y, z + 2, k), recv_of(z + 2))
-    send(blk(y, z + 2, k), blk(y, z + 2, k), recv_of(z + 2), dev(y, z - 1, k))
-    for off in (-1, 1):
-        wait(blk(y, z + off, k), recv_of(z + off))
-        spread(off)
-    spread(-2)
-    spread(2)
-    for off in (-3, 3, -4):
-        wait(blk(y, z + off, k), recv_of(z + off))
-        spread(off)
+    for s in range(4):
+        if s >= 1:
+            wait(blk(y, z - s, k), recv_of(z - s))
+        send(x_ref if s == 0 else blk(y, z - s, k), blk(y, z - s, k), recv_of(z - s), zr)
+        if s < 3:
+            if s >= 1:
+                wait(blk(y, z + s, k), recv_of(z + s))
+            send(x_ref if s == 0 else blk(y, z + s, k), blk(y, z + s, k), recv_of(z + s), zl)
+        if s == 0:
+            spread(0)
+        else:
+            spread(-s)
+            if s < 3:
+                spread(s)
+    wait(blk(y, z - 4, k), recv_of(z - 4))
+    spread(-4)
+    wait(blk(y, z + 3, k), recv_of(z + 3))
+    spread(3)
     local.wait()
     if mode != "first":
         for i, off in enumerate(offs):

time: 190 us -> 197 us (1.037)
  Pallas kernels: 180 us -> 186 us
    pallas_call x4, Pallas kernels: 130 us -> 137 us  [gather_product(): pl.pallas_call(functools.partial(gather_kernel, mode='fused', which=which...]
where the time goes in v15:
time: 197 us
  Pallas kernels  186 us (94%)
  other arithmetic  6.67 us (3%)
  local copies, waits for them, and re-layouts  2.14 us (1%)
    pallas_call x4, Pallas kernels, gather_product(): pl.pallas_call(functools.partial(gather_kernel, mode='fused', which=which...  137 us
    pallas_call x1, Pallas kernels, first_product(): pl.pallas_call(functools.partial(gather_kernel, mode='first', which=0), o...  49 us

profile of v15, /device:TPU:1, one launch (start us, length us, event | category | flops | bytes accessed | tf_op | source)
XLA Modules:
  0.0 196.5 jit_solution(2703574372137201233)
XLA Ops:
  0.0 0.7 select_reduce_fusion
  0.7 0.7 slice.3
  1.5 0.1 convert_reduce_fusion
  1.6 0.7 fusion
  3.6 0.7 iota_compare_fusion.3
  4.3 0.8 select_reduce_fusion.2
  5.1 0.7 select_reduce_fusion.4
  5.8 0.7 select_reduce_fusion.3
  6.6 0.7 compare_bitcast_fusion
  7.3 0.6 reshape.76.refs_3_
  7.9 0.1 broadcast_bitcast_fusion
  8.0 0.7 copy.9
  8.7 49.0 %shard_map.64 = (f32[128,128]{1,0:T(8,128)}, f32[128,8192]{1,0:T(8,128)}) custom-call(f32[128,128]{1,0:T(8,128)} %refs_4_.1, f32[128,2048]{1,0:T(8,128)} %refs_1_.1, f32[2,8192]{1,0:T(2,128)} %bitcast.9, f32[3,128]{1,0:T(4,128)} %reshape.76.refs_3_), custom_call_target="tpu_custom_call" | custom-call | flops 268435456 | bytes 16777216 | tf_op jit(solution)/shard_map/pallas_call | solution.py:237
  57.7 36.6 %shard_map.65 = (f32[128,128]{1,0:T(8,128)}, f32[128,128]{1,0:T(8,128)}) custom-call(f32[128,128]{1,0:T(8,128)} %get-tuple-element.12.refs_0_.refs_4_, f32[128,8192]{1,0:T(8,128)} %get-tuple-element.13.refs_1_, f32[2,8192]{1,0:T(2,128)} %bitcast.10, f32[128,128]{1,0:T(8,128)} %refs_4_.1), custom_call_target="tpu_custom_call" | custom-call | flops 268435456 | bytes 12582912 | tf_op jit(solution)/shard_map/pallas_call | solution.py:256
  94.3 32.7 %shard_map.66 = (f32[128,128]{1,0:T(8,128)}, f32[128,128]{1,0:T(8,128)}) custom-call(f32[128,128]{1,0:T(8,128)} %get-tuple-element.14.refs_0_, f32[128,8192]{1,0:T(8,128)} %get-tuple-element.13.refs_1_, f32[2,8192]{1,0:T(2,128)} %bitcast.11, f32[3,128]{1,0:T(4,128)} %reshape.76.refs_3_, f32[128,128]{1,0:T(8,128)} %get-tuple-element.12.refs_0_.refs_4_), custom_call_target="tpu_custom_call" | custom-call | flops 268435456 | bytes 12582912 | tf_op jit(solution)/shard_map/pallas_call | solution.py:256
  127.0 0.0 copy-start
  127.0 33.9 %shard_map.67 = (f32[128,128]{1,0:T(8,128)}, f32[128,128]{1,0:T(8,128)}) custom-call(f32[128,128]{1,0:T(8,128)} %get-tuple-element.16.refs_0_, f32[128,8192]{1,0:T(8,128)} %get-tuple-element.13.refs_1_, f32[2,8192]{1,0:T(2,128)} %bitcast.12, f32[128,128]{1,0:T(8,128)} %get-tuple-element.17.refs_3_, f32[128,128]{1,0:T(8,128)} %refs_4_.1), custom_call_target="tpu_custom_call" | custom-call | flops 268435456 | bytes 12582912 | tf_op jit(solution)/shard_map/pallas_call | solution.py:256
  160.9 34.1 %shard_map.68 = f32[128,128]{1,0:T(8,128)} custom-call(f32[128,128]{1,0:T(8,128)} %get-tuple-element.18.refs_0_, f32[128,8192]{1,0:T(8,128)} %get-tuple-element.13.refs_1_, f32[2,8192]{1,0:T(2,128)} %bitcast.13, f32[3,128]{1,0:T(4,128)} %reshape.76.refs_3_), custom_call_target="tpu_custom_call" | custom-call | flops 268435456 | bytes 12582912 | tf_op jit(solution)/shard_map/pallas_call | solution.py:256
  195.1 0.0 copy-done
  195.1 1.5 add.7
  (2 shorter events, 0.0 us)
Async XLA Ops:
  127.0 68.1 %copy-start = (f32[128,128]{1,0:T(8,128)S(1)}, f32[128,128]{1,0:T(8,128)}, u32[]{:S(2)}) copy-start(f32[128,128]{1,0:T(8,128)} %get-tuple-element.15) | copy-start | bytes 196612
